TPU v7x, 512 devices: a whole 4x8x8 slice. The times are simulated.
512 devices in a mesh: board: 8 (over y), sub: 64 (over z, x, core).
Axes of the slice: x: 4, y: 8, z: 8, core: 2. Of those that a mesh axis runs over, the one named last changes fastest.
Arguments:
- rhs: float32 [8, 32, 16384], P('board', None, 'sub')
- schur: float32 [8, 49152, 768], P('board', 'sub'), as said below
- block_list: int32 [8, 384], P('board', 'sub'), may hold values from 0 to 127, as said below
- pad_rows: int32 [8, 4096], P('board', 'sub'), may hold values from 0 to 255, as said below
- pad_cond: float32 [8, 4096], P('board', 'sub'), may hold values from 0.5 to 2
- sink: float32 [8, 16384], P('board', 'sub'), may hold values from 0.2 to 2
- precond: float32 [8, 16384], P('board', 'sub'), may hold values from 0.3 to 1
Outputs:
- solution: float32 [8, 32, 16384], P('board', None, 'sub')
- residual: float32 [8, 32, 16384], P('board', None, 'sub')
Inputs may be any that keep to these rules, and one draw needn't show every extreme that they name: `block_list`: every entry of a subdomain s's list is a block owned by a subdomain at most 3 away from s on the same board; the entries of one list are different and rising, and include all blocks that s owns. `pad_rows`: A subdomain's pad rows are different and rising, and include its first and last owned row. `schur`: each Schur block is symmetric and positive definite.
All inputs are finite; a program needn't handle non-finite values.
Results may differ from a plain program's by a relative error of at most 0.0003.
Values sent between devices are 32-bit elements; how exact they have to be, the bound alone decides.
A program may use at most 64 MiB of HBM per device.

v0:
```python
import jax
import jax.numpy as jnp
from jax import lax
from jax.sharding import PartitionSpec as P

BR = 128
REACH = 3
ITERS = 2


def passed_along(value, axis, steps):
    count = lax.axis_size(axis)
    leading, last = (max(0, -steps), min(count, count - steps))
    return lax.ppermute(value, axis, [(source, source + steps) for source in range(leading, last)])


def from_partner(shard, axis, bit):
    return lax.ppermute(shard, axis, [(i, i ^ 1 << bit) for i in range(lax.axis_size(axis))])


def case_sums(left, right):
    return jnp.sum(left * right, axis=1)


def on_device(rhs, schur, block_list, pad_rows, pad_cond, sink, precond):
    right_side = rhs[0]
    matrix = schur[0]
    block_ids = block_list[0]
    pad_local = pad_rows[0]
    conduct = pad_cond[0]
    sink_rows = sink[0][None, :]
    scaling = precond[0][None, :]
    cases = right_side.shape[0]
    owned_rows = right_side.shape[1]
    blocks_owned = owned_rows // BR
    inner = matrix.shape[0]
    touched = block_ids.shape[0]
    position = lax.axis_index("sub")
    shifted_ids = block_ids - (position - REACH) * blocks_owned
    solution = jnp.zeros_like(right_side)
    residual = right_side
    precon = scaling * residual
    direction = precon
    norm_now = lax.psum(case_sums(residual, precon), ("board", "sub"))
    for iteration in range(ITERS):
        segments = []
        for offset in range(-REACH, REACH + 1):
            if offset == 0:
                segments.append(direction)
            else:
                segments.append(passed_along(direction, "sub", -offset))
        apply_blocks = jnp.concatenate(segments, axis=1).reshape(cases, -1, BR)
        picked = jnp.take(apply_blocks, shifted_ids, axis=1).reshape(cases, inner)
        product = jnp.dot(picked, matrix, precision=lax.Precision.HIGHEST)
        partial_value = (
            jnp.zeros(apply_blocks.shape, jnp.float32)
            .at[:, shifted_ids]
            .add(product.reshape(cases, touched, BR))
        )
        pieces = partial_value.reshape(cases, 2 * REACH + 1, owned_rows)
        result = pieces[:, REACH]
        for offset in range(-REACH, REACH + 1):
            if offset != 0:
                result = result + passed_along(pieces[:, REACH + offset], "sub", offset)
        pad_values = jnp.take(direction, pad_local, axis=1)
        other_values, other_cond = from_partner((pad_values, conduct), "board", 0)
        mean_cond = 0.5 * (conduct + other_cond)
        result = result.at[:, pad_local].add(mean_cond[None, :] * (pad_values - other_values))
        image = result + sink_rows * direction
        final = iteration == ITERS - 1
        curve = lax.psum(case_sums(direction, image), ("board", "sub"))
        alpha = norm_now / curve
        solution = solution + alpha[:, None] * direction
        residual = residual - alpha[:, None] * image
        if not final:
            precon = scaling * residual
            fresh = lax.psum(case_sums(residual, precon), ("board", "sub"))
            direction = precon + (fresh / norm_now)[:, None] * direction
            norm_now = fresh
    return (solution[None], residual[None])


def solution(mesh):
    in_specs = (
        P("board", None, "sub"),
        P("board", "sub", None),
        P("board", "sub"),
        P("board", "sub"),
        P("board", "sub"),
        P("board", "sub"),
        P("board", "sub"),
    )
    out_specs = (P("board", None, "sub"), P("board", None, "sub"))
    return jax.shard_map(
        on_device, mesh=mesh, in_specs=in_specs, out_specs=out_specs, check_vma=False
    )
```

profile of v0, /device:TPU:1, one launch (start us, length us, event | category | flops | bytes accessed | tf_op | source)
XLA Modules:
  0.0 425.5 jit_solution(17108180576712757444)
XLA Ops:
  2.3 6.0 %collective-permute-start = (f32[32,256]{0,1:T(8,128)S(1)}, f32[32,256]{0,1:T(8,128)S(1)}, u32[]{:S(2)}, u32[]{:S(2)}) collective-permute-start(f32[32,256]{0,1:T(8,128)S(1)} %bitcast_multiply_fusion.1), channel_id=1, source_target_pairs={{0,3},{1,4},{2,5},{3,6},{4,7},{5,8},{6,9},{7,10},{8,11},{9,12},{10... | collective-permute-start | bytes 98312 | tf_op jit(solution)/shard_map/ppermute | solution.py:14
  8.3 2.2 collective-permute-start.1
  10.5 2.2 collective-permute-start.2
  12.7 2.2 collective-permute-start.3
  20.8 2.0 copy.104
  25.6 3.1 collective-permute-start.12
  32.7 2.2 convolution_bitcast_fusion.1
  35.6 2.1 scatter_fusion
  39.1 3.9 collective-permute-start.10
  43.6 7.5 %collective-permute-start.11 = (f32[32,256]{0,1:T(8,128)S(1)}, f32[32,256]{0,1:T(8,128)S(1)}, u32[]{:S(2)}, u32[]{:S(2)}) collective-permute-start(f32[32,256]{0,1:T(8,128)S(1)} %get-tuple-element.31), channel_id=1, source_target_pairs={{0,3},{1,4},{2,5},{3,6},{4,7},{5,8},{6,9},{7,10},{8,11},{9,12},{10... | collective-permute-start | bytes 98312 | tf_op jit(solution)/shard_map/ppermute | solution.py:14
  55.6 3.6 collective-permute-start.9
  60.4 3.2 collective-permute-start.13
  66.8 108.5 %all-reduce = (f32[32]{0:T(128)S(1)}, f32[32]{0:T(128)S(1)}) all-reduce(f32[32]{0:T(128)S(1)} %get-tuple-element.17, f32[32]{0:T(128)S(1)} %get-tuple-element.16), channel_id=1, replica_groups=mesh['board'=8,'sub'=64] {'board','sub'}, use_global_device_ids=true, to_apply=%region_1.0 | all-reduce | flops 64 | bytes 512 | tf_op jit(solution)/shard_map/psum | solution.py:44
  175.5 94.4 %psum.30 = f32[32]{0:T(128)S(1)} all-reduce(f32[32]{0:T(128)S(1)} %get-tuple-element.20), channel_id=1, replica_groups=mesh['board'=8,'sub'=64] {'board','sub'}, use_global_device_ids=true, to_apply=%region_7.10 | all-reduce | flops 32 | bytes 256 | tf_op jit(solution)/shard_map/psum | solution.py:77
  270.5 3.4 collective-permute-start.14
  274.0 4.0 collective-permute-start.15
  279.9 2.4 collective-permute-start.17
  293.7 2.2 convolution_bitcast_fusion
  302.2 3.6 collective-permute-start.23
  305.9 5.5 %collective-permute-start.24 = (f32[32,256]{0,1:T(8,128)S(1)}, f32[32,256]{0,1:T(8,128)S(1)}, u32[]{:S(2)}, u32[]{:S(2)}) collective-permute-start(f32[32,256]{0,1:T(8,128)S(1)} %get-tuple-element.26), channel_id=1, source_target_pairs={{0,2},{1,3},{2,4},{3,5},{4,6},{5,7},{6,8},{7,9},{8,10},{9,11},{10,... | collective-permute-start | bytes 98312 | tf_op jit(solution)/shard_map/ppermute | solution.py:14
  311.4 5.2 %collective-permute-start.25 = (f32[32,256]{0,1:T(8,128)S(1)}, f32[32,256]{0,1:T(8,128)S(1)}, u32[]{:S(2)}, u32[]{:S(2)}) collective-permute-start(f32[32,256]{0,1:T(8,128)S(1)} %get-tuple-element.25), channel_id=1, source_target_pairs={{0,3},{1,4},{2,5},{3,6},{4,7},{5,8},{6,9},{7,10},{8,11},{9,12},{10... | collective-permute-start | bytes 98312 | tf_op jit(solution)/shard_map/ppermute | solution.py:14
  316.7 1.9 collective-permute-start.26
  319.6 2.1 collective-permute-done.26
  322.9 101.1 %psum.31 = f32[32]{0:T(128)S(1)} all-reduce(f32[32]{0:T(128)S(1)} %multiply_reduce_fusion), channel_id=1, replica_groups=mesh['board'=8,'sub'=64] {'board','sub'}, use_global_device_ids=true, to_apply=%region_11.14 | all-reduce | flops 32 | bytes 256 | tf_op jit(solution)/shard_map/psum | solution.py:71
  (135 shorter events, 49.4 us)
Async XLA Ops:
  2.3 20.6 %collective-permute-start = (f32[32,256]{0,1:T(8,128)S(1)}, f32[32,256]{0,1:T(8,128)S(1)}, u32[]{:S(2)}, u32[]{:S(2)}) collective-permute-start(f32[32,256]{0,1:T(8,128)S(1)} %bitcast_multiply_fusion.1), channel_id=1, source_target_pairs={{0,3},{1,4},{2,5},{3,6},{4,7},{5,8},{6,9},{7,10},{8,11},{9,12},{10... | collective-permute-start | bytes 98312 | tf_op jit(solution)/shard_map/ppermute | solution.py:14
  8.3 17.3 %collective-permute-start.1 = (f32[32,256]{0,1:T(8,128)S(1)}, f32[32,256]{0,1:T(8,128)S(1)}, u32[]{:S(2)}, u32[]{:S(2)}) collective-permute-start(f32[32,256]{0,1:T(8,128)S(1)} %bitcast_multiply_fusion.1), channel_id=1, source_target_pairs={{0,2},{1,3},{2,4},{3,5},{4,6},{5,7},{6,8},{7,9},{8,10},{9,11},{10,... | collective-permute-start | bytes 98312 | tf_op jit(solution)/shard_map/ppermute | solution.py:14
  10.5 19.6 %collective-permute-start.2 = (f32[32,256]{0,1:T(8,128)S(1)}, f32[32,256]{0,1:T(8,128)S(1)}, u32[]{:S(2)}, u32[]{:S(2)}) collective-permute-start(f32[32,256]{0,1:T(8,128)S(1)} %bitcast_multiply_fusion.1), channel_id=1, source_target_pairs={{0,1},{1,2},{2,3},{3,4},{4,5},{5,6},{6,7},{7,8},{8,9},{9,10},{10,1... | collective-permute-start | bytes 98312 | tf_op jit(solution)/shard_map/ppermute | solution.py:14
  12.7 17.6 %collective-permute-start.3 = (f32[32,256]{0,1:T(8,128)S(1)}, f32[32,256]{0,1:T(8,128)S(1)}, u32[]{:S(2)}, u32[]{:S(2)}) collective-permute-start(f32[32,256]{0,1:T(8,128)S(1)} %bitcast_multiply_fusion.1), channel_id=1, source_target_pairs={{1,0},{2,1},{3,2},{4,3},{5,4},{6,5},{7,6},{8,7},{9,8},{10,9},{11,1... | collective-permute-start | bytes 98312 | tf_op jit(solution)/shard_map/ppermute | solution.py:14
  15.0 15.4 %collective-permute-start.4 = (f32[32,256]{0,1:T(8,128)S(1)}, f32[32,256]{0,1:T(8,128)S(1)}, u32[]{:S(2)}, u32[]{:S(2)}) collective-permute-start(f32[32,256]{0,1:T(8,128)S(1)} %bitcast_multiply_fusion.1), channel_id=1, source_target_pairs={{2,0},{3,1},{4,2},{5,3},{6,4},{7,5},{8,6},{9,7},{10,8},{11,9},{12,... | collective-permute-start | bytes 98312 | tf_op jit(solution)/shard_map/ppermute | solution.py:14
  22.9 8.9 %collective-permute-start.5 = (f32[32,256]{0,1:T(8,128)S(1)}, f32[32,256]{0,1:T(8,128)S(1)}, u32[]{:S(2)}, u32[]{:S(2)}) collective-permute-start(f32[32,256]{0,1:T(8,128)S(1)} %bitcast_multiply_fusion.1), channel_id=1, source_target_pairs={{3,0},{4,1},{5,2},{6,3},{7,4},{8,5},{9,6},{10,7},{11,8},{12,9},{13... | collective-permute-start | bytes 98312 | tf_op jit(solution)/shard_map/ppermute | solution.py:14
  25.6 28.0 %collective-permute-start.12 = (f32[64]{0:T(128)}, f32[64]{0:T(128)}, u32[]{:S(2)}, u32[]{:S(2)}) collective-permute-start(f32[64]{0:T(128)} %bitcast.155), channel_id=1, source_target_pairs={{0,64},{64,0},{128,192},{192,128},{256,320},{320,256},{384,448},{4... | collective-permute-start | bytes 776 | tf_op jit(solution)/shard_map/ppermute | solution.py:18
  39.1 16.5 %collective-permute-start.10 = (f32[32,256]{0,1:T(8,128)S(1)}, f32[32,256]{0,1:T(8,128)S(1)}, u32[]{:S(2)}, u32[]{:S(2)}) collective-permute-start(f32[32,256]{0,1:T(8,128)S(1)} %get-tuple-element.32), channel_id=1, source_target_pairs={{0,2},{1,3},{2,4},{3,5},{4,6},{5,7},{6,8},{7,9},{8,10},{9,11},{10,... | collective-permute-start | bytes 98312 | tf_op jit(solution)/shard_map/ppermute | solution.py:14
  43.6 16.9 %collective-permute-start.11 = (f32[32,256]{0,1:T(8,128)S(1)}, f32[32,256]{0,1:T(8,128)S(1)}, u32[]{:S(2)}, u32[]{:S(2)}) collective-permute-start(f32[32,256]{0,1:T(8,128)S(1)} %get-tuple-element.31), channel_id=1, source_target_pairs={{0,3},{1,4},{2,5},{3,6},{4,7},{5,8},{6,9},{7,10},{8,11},{9,12},{10... | collective-permute-start | bytes 98312 | tf_op jit(solution)/shard_map/ppermute | solution.py:14
  51.0 12.6 %collective-permute-start.6 = (f32[32,256]{0,1:T(8,128)S(1)}, f32[32,256]{0,1:T(8,128)S(1)}, u32[]{:S(2)}, u32[]{:S(2)}) collective-permute-start(f32[32,256]{0,1:T(8,128)S(1)} %get-tuple-element.30), channel_id=1, source_target_pairs={{3,0},{4,1},{5,2},{6,3},{7,4},{8,5},{9,6},{10,7},{11,8},{12,9},{13... | collective-permute-start | bytes 98312 | tf_op jit(solution)/shard_map/ppermute | solution.py:14
  52.3 11.3 %collective-permute-start.7 = (f32[32,256]{0,1:T(8,128)S(1)}, f32[32,256]{0,1:T(8,128)S(1)}, u32[]{:S(2)}, u32[]{:S(2)}) collective-permute-start(f32[32,256]{0,1:T(8,128)S(1)} %get-tuple-element.35), channel_id=1, source_target_pairs={{2,0},{3,1},{4,2},{5,3},{6,4},{7,5},{8,6},{9,7},{10,8},{11,9},{12,... | collective-permute-start | bytes 98312 | tf_op jit(solution)/shard_map/ppermute | solution.py:14
  53.6 10.0 %collective-permute-start.8 = (f32[32,256]{0,1:T(8,128)S(1)}, f32[32,256]{0,1:T(8,128)S(1)}, u32[]{:S(2)}, u32[]{:S(2)}) collective-permute-start(f32[32,256]{0,1:T(8,128)S(1)} %get-tuple-element.34), channel_id=1, source_target_pairs={{1,0},{2,1},{3,2},{4,3},{5,4},{6,5},{7,6},{8,7},{9,8},{10,9},{11,1... | collective-permute-start | bytes 98312 | tf_op jit(solution)/shard_map/ppermute | solution.py:14
  55.6 8.1 %collective-permute-start.9 = (f32[32,256]{0,1:T(8,128)S(1)}, f32[32,256]{0,1:T(8,128)S(1)}, u32[]{:S(2)}, u32[]{:S(2)}) collective-permute-start(f32[32,256]{0,1:T(8,128)S(1)} %get-tuple-element.33), channel_id=1, source_target_pairs={{0,1},{1,2},{2,3},{3,4},{4,5},{5,6},{6,7},{7,8},{8,9},{9,10},{10,1... | collective-permute-start | bytes 98312 | tf_op jit(solution)/shard_map/ppermute | solution.py:14
  270.5 13.1 %collective-permute-start.14 = (f32[32,256]{0,1:T(8,128)S(1)}, f32[32,256]{0,1:T(8,128)S(1)}, u32[]{:S(2)}, u32[]{:S(2)}) collective-permute-start(f32[32,256]{0,1:T(8,128)S(1)} %multiply_add_fusion), channel_id=1, source_target_pairs={{0,3},{1,4},{2,5},{3,6},{4,7},{5,8},{6,9},{7,10},{8,11},{9,12},{10... | collective-permute-start | bytes 98312 | tf_op jit(solution)/shard_map/ppermute | solution.py:14
  274.0 12.4 %collective-permute-start.15 = (f32[32,256]{0,1:T(8,128)S(1)}, f32[32,256]{0,1:T(8,128)}, u32[]{:S(2)}, u32[]{:S(2)}) collective-permute-start(f32[32,256]{0,1:T(8,128)S(1)} %multiply_add_fusion), channel_id=1, source_target_pairs={{0,2},{1,3},{2,4},{3,5},{4,6},{5,7},{6,8},{7,9},{8,10},{9,11},{10,... | collective-permute-start | bytes 98312 | tf_op jit(solution)/shard_map/ppermute | solution.py:14
  277.9 10.8 %collective-permute-start.16 = (f32[32,256]{0,1:T(8,128)S(1)}, f32[32,256]{0,1:T(8,128)S(1)}, u32[]{:S(2)}, u32[]{:S(2)}) collective-permute-start(f32[32,256]{0,1:T(8,128)S(1)} %multiply_add_fusion), channel_id=1, source_target_pairs={{0,1},{1,2},{2,3},{3,4},{4,5},{5,6},{6,7},{7,8},{8,9},{9,10},{10,1... | collective-permute-start | bytes 98312 | tf_op jit(solution)/shard_map/ppermute | solution.py:14
  279.9 10.3 %collective-permute-start.17 = (f32[32,256]{0,1:T(8,128)S(1)}, f32[32,256]{0,1:T(8,128)S(1)}, u32[]{:S(2)}, u32[]{:S(2)}) collective-permute-start(f32[32,256]{0,1:T(8,128)S(1)} %multiply_add_fusion), channel_id=1, source_target_pairs={{1,0},{2,1},{3,2},{4,3},{5,4},{6,5},{7,6},{8,7},{9,8},{10,9},{11,1... | collective-permute-start | bytes 98312 | tf_op jit(solution)/shard_map/ppermute | solution.py:14
  283.7 8.5 %collective-permute-start.19 = (f32[32,256]{0,1:T(8,128)S(1)}, f32[32,256]{0,1:T(8,128)S(1)}, u32[]{:S(2)}, u32[]{:S(2)}) collective-permute-start(f32[32,256]{0,1:T(8,128)S(1)} %multiply_add_fusion), channel_id=1, source_target_pairs={{3,0},{4,1},{5,2},{6,3},{7,4},{8,5},{9,6},{10,7},{11,8},{12,9},{13... | collective-permute-start | bytes 98312 | tf_op jit(solution)/shard_map/ppermute | solution.py:14
  297.1 14.3 %collective-permute-start.20 = (f32[32,256]{0,1:T(8,128)S(1)}, f32[32,256]{0,1:T(8,128)S(1)}, u32[]{:S(2)}, u32[]{:S(2)}) collective-permute-start(f32[32,256]{0,1:T(8,128)S(1)} %get-tuple-element.24), channel_id=1, source_target_pairs={{3,0},{4,1},{5,2},{6,3},{7,4},{8,5},{9,6},{10,7},{11,8},{12,9},{13... | collective-permute-start | bytes 98312 | tf_op jit(solution)/shard_map/ppermute | solution.py:14
  299.0 17.6 %collective-permute-start.21 = (f32[32,256]{0,1:T(8,128)S(1)}, f32[32,256]{0,1:T(8,128)S(1)}, u32[]{:S(2)}, u32[]{:S(2)}) collective-permute-start(f32[32,256]{0,1:T(8,128)S(1)} %get-tuple-element.29), channel_id=1, source_target_pairs={{2,0},{3,1},{4,2},{5,3},{6,4},{7,5},{8,6},{9,7},{10,8},{11,9},{12,... | collective-permute-start | bytes 98312 | tf_op jit(solution)/shard_map/ppermute | solution.py:14
  300.3 18.3 %collective-permute-start.22 = (f32[32,256]{0,1:T(8,128)S(1)}, f32[32,256]{0,1:T(8,128)S(1)}, u32[]{:S(2)}, u32[]{:S(2)}) collective-permute-start(f32[32,256]{0,1:T(8,128)S(1)} %get-tuple-element.28), channel_id=1, source_target_pairs={{1,0},{2,1},{3,2},{4,3},{5,4},{6,5},{7,6},{8,7},{9,8},{10,9},{11,1... | collective-permute-start | bytes 98312 | tf_op jit(solution)/shard_map/ppermute | solution.py:14
  302.2 16.4 %collective-permute-start.23 = (f32[32,256]{0,1:T(8,128)S(1)}, f32[32,256]{0,1:T(8,128)S(1)}, u32[]{:S(2)}, u32[]{:S(2)}) collective-permute-start(f32[32,256]{0,1:T(8,128)S(1)} %get-tuple-element.27), channel_id=1, source_target_pairs={{0,1},{1,2},{2,3},{3,4},{4,5},{5,6},{6,7},{7,8},{8,9},{9,10},{10,1... | collective-permute-start | bytes 98312 | tf_op jit(solution)/shard_map/ppermute | solution.py:14
  305.9 12.7 %collective-permute-start.24 = (f32[32,256]{0,1:T(8,128)S(1)}, f32[32,256]{0,1:T(8,128)S(1)}, u32[]{:S(2)}, u32[]{:S(2)}) collective-permute-start(f32[32,256]{0,1:T(8,128)S(1)} %get-tuple-element.26), channel_id=1, source_target_pairs={{0,2},{1,3},{2,4},{3,5},{4,6},{5,7},{6,8},{7,9},{8,10},{9,11},{10,... | collective-permute-start | bytes 98312 | tf_op jit(solution)/shard_map/ppermute | solution.py:14
  311.4 8.0 %collective-permute-start.25 = (f32[32,256]{0,1:T(8,128)S(1)}, f32[32,256]{0,1:T(8,128)S(1)}, u32[]{:S(2)}, u32[]{:S(2)}) collective-permute-start(f32[32,256]{0,1:T(8,128)S(1)} %get-tuple-element.25), channel_id=1, source_target_pairs={{0,3},{1,4},{2,5},{3,6},{4,7},{5,8},{6,9},{7,10},{8,11},{9,12},{10... | collective-permute-start | bytes 98312 | tf_op jit(solution)/shard_map/ppermute | solution.py:14
  (16 other events, 511.9 us)
where the time goes:
time: 427 us; the launch traced here: 426 us
  blocking collectives  304 us (71%)
  starting transfers between devices  76.1 us (18%)
  local copies, waits for them, and re-layouts  18.5 us (4%)
  other arithmetic  14.1 us (3%)
  waiting for transfers between devices  6.94 us (2%)
  matrix products  4.43 us (1%)
    psum x1, blocking collectives, on_device(): norm_now = lax.psum(case_sums(residual, precon), ('board', 'sub'))  108 us
    psum x1, blocking collectives, on_device(): curve = lax.psum(case_sums(direction, image), ('board', 'sub'))  101 us
    psum x1, blocking collectives, on_device(): fresh = lax.psum(case_sums(residual, precon), ('board', 'sub'))  94.4 us
    ppermute x24, starting transfers between devices, passed_along(): lax.ppermute(value, axis, [(source, source + steps) for source in range(l...  67.9 us
    unnamed x42, local copies, waits for them, and re-layouts  8.71 us
  transfers between devices with their start and end apart: 27, of which 5 were waited for; matrix products, arithmetic and copies ran while one was open for 6% of the time, Pallas kernels for 0%

commit v1 on v0

v1 whole, which is shorter than its diff:
```python
import functools

import jax
import jax.numpy as jnp
from jax import lax
from jax.experimental import pallas as pl
from jax.experimental.pallas import tpu as pltpu
from jax.sharding import PartitionSpec as P

BR = 128
REACH = 3
OFFSETS = (3, -3, 2, -2, 1, -1)
F32 = jnp.float32
BF16 = jnp.bfloat16


def split(value):
    high = value.astype(BF16)
    low = (value - high.astype(F32)).astype(BF16)
    return high, low


def kernel(
    n_board, n_sub,
    rhs, schur, blocks, pad_rows, pad_cond, sink, precond,
    x_out, r_out,
    b_own, s_full, s_high, s_low, one_hot, pad_out, pad_in, pad_keep,
    halo, prod, parts, back, image_own, group_a, group_b,
    load_sem, halo_send, halo_recv, back_send, back_recv, pad_send, pad_recv,
    a_send, a_recv, b_send, b_recv,
):
    me_b = lax.axis_index("board")
    me_s = lax.axis_index("sub")
    core = lax.rem(me_s, 2)
    chip = lax.div(me_s, 2)
    n_a, n_chip = 2 * n_board, n_sub // 2
    a_id = me_b * 2 + core
    partner = me_b + 1 - 2 * lax.rem(me_b, 2)
    touched = blocks.shape[1]
    inner = schur.shape[1]

    def near(offset):
        return (me_b, lax.rem(me_s + offset + n_sub, n_sub))

    def in_a(step):
        other = lax.rem(a_id + step, n_a)
        return (lax.div(other, 2), 2 * chip + lax.rem(other, 2))

    def in_b(step):
        return (me_b, 2 * lax.rem(chip + step, n_chip) + core)

    loads = [
        pltpu.make_async_copy(rhs.at[0, :, pl.ds(BR * i, BR)], b_own.at[i], load_sem.at[i])
        for i in range(2)
    ]
    rows = inner // 6
    for i in range(6):
        cut = pl.ds(rows * i, rows)
        loads.append(pltpu.make_async_copy(schur.at[0, cut], s_full.at[cut], load_sem.at[2 + i]))
    for load in loads:
        load.start()

    barrier = pltpu.get_barrier_semaphore()

    def greet(device):
        pl.semaphore_signal(barrier, inc=1, device_id=device, device_id_type=pl.DeviceIdType.MESH)

    for offset in (3, -3):
        greet(near(offset))
    greet((me_b, lax.rem(me_s + 2 * core - 1 + n_sub, n_sub)))
    for step in range(1, n_a):
        greet(in_a(step))
    for step in range(1, n_chip):
        greet(in_b(step))

    loads[0].wait()
    loads[1].wait()
    scale = [precond[0:1, BR * i : BR * (i + 1)] for i in range(2)]
    leak = [sink[0:1, BR * i : BR * (i + 1)] for i in range(2)]
    for i in range(2):
        halo[0, 2 * REACH + i] = scale[i] * b_own[i]
    pad_out[...] = jnp.zeros_like(pad_out)
    prod[touched] = jnp.zeros_like(prod[touched])
    n_pads = pad_rows.shape[1]
    row_ids = lax.broadcasted_iota(jnp.int32, (2 * BR, n_pads), 0)
    one_hot[...] = jnp.zeros_like(one_hot)
    one_hot[:, :n_pads] = jnp.where(row_ids == pad_rows[...], 1.0, 0.0).astype(BF16)

    def pads_of(slot):
        high, low = split(jnp.concatenate([halo[slot, 2 * REACH], halo[slot, 2 * REACH + 1]], axis=1))
        both = jnp.dot(jnp.concatenate([high, low], axis=0), one_hot[...], preferred_element_type=F32)
        return both[:32] + both[32:]

    own_pads = pads_of(0)
    pad_out[0, :32] = own_pads
    pad_out[0, 32:33, :n_pads] = pad_cond[...]
    last = 2 * (2 * REACH + 1) - 1
    index = [jnp.clip(blocks[0, j] - (me_s - REACH) * 2, 0, last) for j in range(touched)]
    inverse = []
    for k in range(2 * (2 * REACH + 1)):
        where = jnp.int32(touched)
        for j in range(touched):
            where = jnp.where(index[j] == k, j, where)
        inverse.append(where)

    pl.semaphore_wait(barrier, 3 + n_a - 1 + n_chip - 1)

    sent = []

    def send(source, target, send_sem, recv_sem, device):
        copy = pltpu.make_async_remote_copy(
            src_ref=source, dst_ref=target, send_sem=send_sem, recv_sem=recv_sem,
            device_id=device, device_id_type=pl.DeviceIdType.MESH,
        )
        copy.start()
        sent.append(copy)
        return copy

    def send_halo(slot):
        copies = []
        for n, offset in enumerate(OFFSETS):
            copies.append(send(
                halo.at[slot, pl.ds(2 * REACH, 2)], halo.at[slot, pl.ds(2 * (REACH - offset), 2)],
                halo_send.at[slot, n], halo_recv.at[slot, n], near(offset)))
        copies.append(send(pad_out.at[slot], pad_in.at[slot], pad_send.at[slot], pad_recv.at[slot], (partner, me_s)))
        return copies

    def send_back(slot):
        copies = []
        for n, offset in enumerate(OFFSETS):
            copies.append(send(
                parts.at[slot, pl.ds(2 * (REACH + offset), 2)], back.at[slot, n],
                back_send.at[slot, n], back_recv.at[slot, n], near(offset)))
        return copies

    def apply(slot):
        picked = [halo[slot, index[j]] for j in range(touched)]
        splits = [split(block) for block in picked]
        high = jnp.concatenate([pair[0] for pair in splits], axis=1)
        low = jnp.concatenate([pair[1] for pair in splits], axis=1)
        both = jnp.dot(jnp.concatenate([high, low], axis=0), s_high[...], preferred_element_type=F32)
        product = both[:32] + both[32:] + jnp.dot(high, s_low[...], preferred_element_type=F32)
        return picked, [product[:, BR * j : BR * (j + 1)] for j in range(touched)]

    def put_parts(slot, product):
        for j in range(touched):
            prod[j] = product[j]
        for k in range(2 * (2 * REACH + 1)):
            parts[slot, k] = prod[inverse[k]]

    def collect(slot, copies, coupling):
        high, low = split(coupling)
        both = lax.dot_general(
            jnp.concatenate([high, low], axis=0), one_hot[...], (((1,), (1,)), ((), ())), preferred_element_type=F32)
        spread = both[:32] + both[32:]
        for copy in copies:
            copy.wait_recv()
        result = []
        for i in range(2):
            total = parts[slot, 2 * REACH + i]
            for n in range(len(OFFSETS)):
                total = total + back[slot, n, i]
            total = total + spread[:, BR * i : BR * (i + 1)]
            result.append(total + leak[i] * halo[slot, 2 * REACH + i])
        return result

    def start_sum(slot, terms):
        stacked = jnp.concatenate(terms, axis=0)
        row = jnp.sum(stacked.T, axis=0, keepdims=True)
        group_a[slot, a_id] = row
        return [
            send(group_a.at[slot, a_id], group_a.at[slot, a_id],
                 a_send.at[slot, step - 1], a_recv.at[slot, step - 1], in_a(step))
            for step in range(1, n_a)
        ]

    def mid_sum(slot, copies):
        for copy in copies:
            copy.wait_recv()
        group_b[slot, chip] = jnp.sum(group_a[slot], axis=0)
        return [
            send(group_b.at[slot, chip], group_b.at[slot, chip],
                 b_send.at[slot, step - 1], b_recv.at[slot, step - 1], in_b(step))
            for step in range(1, n_chip)
        ]

    def end_sum(slot, copies):
        for copy in copies:
            copy.wait_recv()
        row = jnp.sum(group_b[slot], axis=0)
        return jnp.broadcast_to(row, (128, 128)).T

    halo_copies = send_halo(0)
    for i in range(6):
        loads[2 + i].wait()
        cut = pl.ds(rows * i, rows)
        high, low = split(s_full[cut])
        s_high[cut] = high
        s_low[cut] = low
    halo_copies[-1].wait_recv()
    mean_cond = 0.5 * (pad_out[0, 32:33] + pad_in[0, 32:33])
    coupling0 = mean_cond * (own_pads - pad_in[0, :32])
    for copy in halo_copies[:-1]:
        copy.wait_recv()
    picked0, product0 = apply(0)
    put_parts(0, product0)
    back_copies = send_back(0)
    curve = own_pads * coupling0
    start = jnp.zeros_like(curve)
    for j in range(touched):
        curve = curve + picked0[j] * product0[j]
    for i in range(2):
        direction = halo[0, 2 * REACH + i]
        curve = curve + leak[i] * direction * direction
        start = start + b_own[i] * direction
    sums = start_sum(0, [start, curve, jnp.zeros_like(curve), jnp.zeros_like(curve)])

    image = collect(0, back_copies, coupling0)
    for i in range(2):
        image_own[i] = image[i]
        halo[1, 2 * REACH + i] = scale[i] * image[i]
    own_pads1 = pads_of(1)
    pad_out[1, :32] = own_pads1
    halo_copies = send_halo(1)
    sums = mid_sum(0, sums)
    for copy in halo_copies:
        copy.wait_recv()
    picked1, product1 = apply(1)
    put_parts(1, product1)
    coupling1 = mean_cond * (own_pads1 - pad_in[1, :32])
    total = end_sum(0, sums)
    norm0, curve0 = total[:32], total[32:64]
    alpha0 = norm0 / curve0
    pads_z = own_pads - alpha0 * own_pads1
    curve = pads_z * (coupling0 - alpha0 * coupling1)
    for j in range(touched):
        curve = curve + (picked0[j] - alpha0 * picked1[j]) * (product0[j] - alpha0 * product1[j])
    fresh = jnp.zeros_like(curve)
    cross = jnp.zeros_like(curve)
    for i in range(2):
        residual = b_own[i] - alpha0 * image_own[i]
        z = scale[i] * residual
        fresh = fresh + residual * z
        cross = cross + z * image_own[i]
        curve = curve + leak[i] * z * z
    sums = start_sum(1, [fresh, curve, cross, jnp.zeros_like(curve)])
    back_copies = send_back(1)
    sums = mid_sum(1, sums)
    image_u = collect(1, back_copies, coupling1)
    total = end_sum(1, sums)
    norm1, zaz, zap = total[:32], total[32:64], total[64:96]
    beta = norm1 / norm0
    alpha1 = norm1 / (zaz + beta * (2.0 * zap + beta * curve0))
    for i in range(2):
        old = halo[0, 2 * REACH + i]
        residual = b_own[i] - alpha0 * image_own[i]
        direction = scale[i] * residual + beta * old
        image1 = (image_own[i] - alpha0 * image_u[i]) + beta * image_own[i]
        x_out[0, :, BR * i : BR * (i + 1)] = alpha0 * old + alpha1 * direction
        r_out[0, :, BR * i : BR * (i + 1)] = residual - alpha1 * image1
    for copy in sent:
        copy.wait_send()


def solution(mesh):
    n_board, n_sub = mesh.shape["board"], mesh.shape["sub"]
    vmem = pl.BlockSpec(memory_space=pltpu.VMEM)
    anywhere = pl.BlockSpec(memory_space=pl.ANY)
    smem = pl.BlockSpec(memory_space=pltpu.SMEM)

    def on_device(rhs, schur, block_list, pad_rows, pad_cond, sink, precond):
        cases, owned = rhs.shape[1:]
        inner = schur.shape[1]
        n_off = len(OFFSETS)
        span = 2 * (2 * REACH + 1)
        dma = pltpu.SemaphoreType.DMA
        out = jax.ShapeDtypeStruct(rhs.shape, F32)
        return pl.pallas_call(
            functools.partial(kernel, n_board, n_sub),
            out_shape=(out, out),
            in_specs=[anywhere, anywhere, smem, vmem, vmem, vmem, vmem],
            out_specs=(vmem, vmem),
            scratch_shapes=[
                pltpu.VMEM((2, cases, BR), F32),
                pltpu.VMEM((inner, inner), F32),
                pltpu.VMEM((inner, inner), BF16),
                pltpu.VMEM((inner, inner), BF16),
                pltpu.VMEM((owned, BR), BF16),
                pltpu.VMEM((2, cases + 8, BR), F32),
                pltpu.VMEM((2, cases + 8, BR), F32),
                pltpu.VMEM((cases, BR), F32),
                pltpu.VMEM((2, span, cases, BR), F32),
                pltpu.VMEM((block_list.shape[1] + 1, cases, BR), F32),
                pltpu.VMEM((2, span, cases, BR), F32),
                pltpu.VMEM((2, n_off, 2, cases, BR), F32),
                pltpu.VMEM((2, cases, BR), F32),
                pltpu.VMEM((2, 2 * n_board, 1, 128), F32),
                pltpu.VMEM((2, n_sub // 2, 1, 128), F32),
                dma((8,)),
                dma((2, n_off)), dma((2, n_off)),
                dma((2, n_off)), dma((2, n_off)),
                dma((2,)), dma((2,)),
                dma((2, 2 * n_board - 1)), dma((2, 2 * n_board - 1)),
                dma((2, n_sub // 2 - 1)), dma((2, n_sub // 2 - 1)),
            ],
            compiler_params=pltpu.CompilerParams(
                collective_id=0, has_side_effects=True, vmem_limit_bytes=32 * 1024 * 1024
            ),
        )(rhs, schur, block_list, pad_rows, pad_cond, sink, precond)

    row = P("board", "sub")
    return jax.shard_map(
        on_device,
        mesh=mesh,
        in_specs=(P("board", None, "sub"), P("board", "sub", None), row, row, row, row, row),
        out_specs=(P("board", None, "sub"), P("board", None, "sub")),
        check_vma=False,
    )
```

time: 427 us -> 55.1 us (0.13)
  blocking collectives: 304 us -> 0 us
  starting transfers between devices: 76.1 us -> 0 us
  Pallas kernels: 0 us -> 47.2 us
  other arithmetic: 14.1 us -> 0 us
  local copies, waits for them, and re-layouts: 18.5 us -> 6.97 us
  waiting for transfers between devices: 6.94 us -> 0 us
  matrix products: 4.43 us -> 0 us
    psum x3 -> x0, blocking collectives: 304 us -> none  [the longest x1 108 us: on_device(): norm_now = lax.psum(case_sums(residual, precon), ('board', 'sub'))]
    ppermute x27 -> x0, starting transfers between devices: 76.1 us -> none  [the longest x24 67.9 us: passed_along(): lax.ppermute(value, axis, [(source, source + steps) for source in range(l...]
    pallas_call x0 -> x1, Pallas kernels: none -> 47.2 us  [on_device(): pl.pallas_call(functools.partial(kernel, n_board, n_sub), out_shape=(out,...]
    ppermute x27 -> x0, waiting for transfers between devices: 6.94 us -> none  [the longest x24 3.94 us: passed_along(): lax.ppermute(value, axis, [(source, source + steps) for source in range(l...]
    scatter-add x4 -> x0, other arithmetic: 5.37 us -> none  [the longest x2 2.88 us: on_device(): partial_value = jnp.zeros(apply_blocks.shape, jnp.float32).at[:, shifted_...]
    ppermute x12 -> x0, local copies, waits for them, and re-layouts: 4.8 us -> none  [passed_along(): lax.ppermute(value, axis, [(source, source + steps) for source in range(l...]
    dot_general x2 -> x0, matrix products: 4.43 us -> none  [on_device(): product = jnp.dot(picked, matrix, precision=lax.Precision.HIGHEST)]
    unnamed x42 -> x16, local copies, waits for them, and re-layouts: 8.71 us -> 6.97 us
  transfers between devices with their start and end apart: 27 -> 0, of which waited for: 5 -> 0; matrix products, arithmetic and copies ran while one was open for 6% -> 0% of each run, Pallas kernels for 0% -> 0%
where the time goes in v1:
time: 55.1 us; the launch traced here: 54.9 us
  Pallas kernels  47.2 us (86%)
  local copies, waits for them, and re-layouts  6.97 us (13%)
  between operations  0.66 us (1%)
    pallas_call x1, Pallas kernels, on_device(): pl.pallas_call(functools.partial(kernel, n_board, n_sub), out_shape=(out,...  47.2 us
    unnamed x16, local copies, waits for them, and re-layouts  6.97 us

profile of v1, /device:TPU:1, one launch (start us, length us, event | category | flops | bytes accessed | tf_op | source)
XLA Modules:
  0.0 54.9 jit_solution(1309809960950258410)
XLA Ops:
  0.6 0.0 copy-start
  0.6 1.7 %copy-done = f32[1,768,768]{2,1,0:T(8,128)S(1)} copy-done((f32[1,768,768]{2,1,0:T(8,128)S(1)}, f32[1,768,768]{2,1,0:T(8,128)}, u32[]{:S(2)}) %copy-start) | copy-done | bytes 2359320
  2.3 0.0 copy-start.1
  2.3 0.8 %copy-done.1 = f32[1,32,256]{2,1,0:T(8,128)S(1)} copy-done((f32[1,32,256]{2,1,0:T(8,128)S(1)}, f32[1,32,256]{2,1,0:T(8,128)}, u32[]{:S(2)}) %copy-start.1) | copy-done | bytes 32792
  3.1 0.0 copy-start.2
  3.1 0.7 %copy-done.2 = f32[1,256]{1,0:T(1,128)S(1)} copy-done((f32[1,256]{1,0:T(1,128)S(1)}, f32[1,256]{1,0:T(1,128)}, u32[]{:S(2)}) %copy-start.2) | copy-done | bytes 1048
  3.7 0.0 copy-start.3
  3.7 0.7 %copy-done.3 = f32[1,256]{1,0:T(1,128)S(1)} copy-done((f32[1,256]{1,0:T(1,128)S(1)}, f32[1,256]{1,0:T(1,128)}, u32[]{:S(2)}) %copy-start.3) | copy-done | bytes 1048
  4.4 0.0 copy-start.4
  4.4 0.7 %copy-done.4 = s32[1,6]{1,0:T(1,128)S(1)} copy-done((s32[1,6]{1,0:T(1,128)S(1)}, s32[1,6]{1,0:T(1,128)}, u32[]{:S(2)}) %copy-start.4) | copy-done | bytes 48
  5.1 0.0 copy-start.5
  5.1 0.7 %copy-done.5 = s32[1,64]{1,0:T(1,128)S(1)} copy-done((s32[1,64]{1,0:T(1,128)S(1)}, s32[1,64]{1,0:T(1,128)}, u32[]{:S(2)}) %copy-start.5) | copy-done | bytes 280
  5.7 0.0 copy-start.6
  5.7 0.7 %copy-done.6 = f32[1,64]{1,0:T(1,128)S(1)} copy-done((f32[1,64]{1,0:T(1,128)S(1)}, f32[1,64]{1,0:T(1,128)}, u32[]{:S(2)}) %copy-start.6) | copy-done | bytes 280
  6.4 47.2 %shard_map.86 = (f32[1,32,256]{2,1,0:T(8,128)S(1)}, f32[1,32,256]{2,1,0:T(8,128)S(1)}) custom-call(f32[1,32,256]{2,1,0:T(8,128)S(1)} %copy-done.1, f32[1,768,768]{2,1,0:T(8,128)S(1)} %copy-done, s32[1,6]{1,0:T(1,128)S(1)} %copy-done.4, s32[1,64]{1,0:T(1,128)S(1)} %copy-done.5, f32[1,64]{1,0:T(1,128)S(1)} %copy-done.6, f32[1,256]{1,0:T(1,128)S(1)} %copy-done.2, ...), custom_call_target="tpu_custom_call" | custom-call | tf_op jit(solution)/shard_map/pallas_call | solution.py:278
  53.6 0.6 %copy.11 = f32[1,32,256]{2,1,0:T(8,128)} copy(f32[1,32,256]{2,1,0:T(8,128)S(1)} %get-tuple-element.4) | data formatting | bytes 65536
  54.2 0.6 %copy.12 = f32[1,32,256]{2,1,0:T(8,128)} copy(f32[1,32,256]{2,1,0:T(8,128)S(1)} %get-tuple-element.5) | data formatting | bytes 65536
Async XLA Ops:
  0.6 1.7 %copy-start = (f32[1,768,768]{2,1,0:T(8,128)S(1)}, f32[1,768,768]{2,1,0:T(8,128)}, u32[]{:S(2)}) copy-start(f32[1,768,768]{2,1,0:T(8,128)} %schur.1) | copy-start | bytes 7077892
  2.3 0.8 %copy-start.1 = (f32[1,32,256]{2,1,0:T(8,128)S(1)}, f32[1,32,256]{2,1,0:T(8,128)}, u32[]{:S(2)}) copy-start(f32[1,32,256]{2,1,0:T(8,128)} %rhs.1) | copy-start | bytes 98308
  3.1 0.7 %copy-start.2 = (f32[1,256]{1,0:T(1,128)S(1)}, f32[1,256]{1,0:T(1,128)}, u32[]{:S(2)}) copy-start(f32[1,256]{1,0:T(1,128)} %sink.1) | copy-start | bytes 3076
  3.7 0.7 %copy-start.3 = (f32[1,256]{1,0:T(1,128)S(1)}, f32[1,256]{1,0:T(1,128)}, u32[]{:S(2)}) copy-start(f32[1,256]{1,0:T(1,128)} %precond.1) | copy-start | bytes 3076
  4.4 0.7 %copy-start.4 = (s32[1,6]{1,0:T(1,128)S(1)}, s32[1,6]{1,0:T(1,128)}, u32[]{:S(2)}) copy-start(s32[1,6]{1,0:T(1,128)} %blocks.1) | copy-start | bytes 76
  5.1 0.7 %copy-start.5 = (s32[1,64]{1,0:T(1,128)S(1)}, s32[1,64]{1,0:T(1,128)}, u32[]{:S(2)}) copy-start(s32[1,64]{1,0:T(1,128)} %pad_rows.1) | copy-start | bytes 772
  5.7 0.7 %copy-start.6 = (f32[1,64]{1,0:T(1,128)S(1)}, f32[1,64]{1,0:T(1,128)}, u32[]{:S(2)}) copy-start(f32[1,64]{1,0:T(1,128)} %pad_cond.1) | copy-start | bytes 772

commit v2 on v1

--- a/solution.py
+++ b/solution.py
@@ -22,9 +22,10 @@
 
 def kernel(
     n_board, n_sub,
-    rhs, schur, blocks, pad_rows, pad_cond, sink, precond,
+    rhs, schur, blocks_in, pad_rows_in, pad_cond_in, sink_in, precond_in,
     x_out, r_out,
-    b_own, s_full, s_high, s_low, one_hot, pad_out, pad_in, pad_keep,
+    blocks, pad_rows, pad_cond, sink, precond,
+    b_own, s_full, s_high, s_low, one_hot, pad_out, pad_in,
     halo, prod, parts, back, image_own, group_a, group_b,
     load_sem, halo_send, halo_recv, back_send, back_recv, pad_send, pad_recv,
     a_send, a_recv, b_send, b_recv,
@@ -53,10 +54,13 @@
         pltpu.make_async_copy(rhs.at[0, :, pl.ds(BR * i, BR)], b_own.at[i], load_sem.at[i])
         for i in range(2)
     ]
+    small = ((precond_in, precond), (pad_rows_in, pad_rows), (blocks_in, blocks), (pad_cond_in, pad_cond), (sink_in, sink))
+    for i, (source, target) in enumerate(small):
+        loads.append(pltpu.make_async_copy(source, target, load_sem.at[2 + i]))
     rows = inner // 6
     for i in range(6):
         cut = pl.ds(rows * i, rows)
-        loads.append(pltpu.make_async_copy(schur.at[0, cut], s_full.at[cut], load_sem.at[2 + i]))
+        loads.append(pltpu.make_async_copy(schur.at[0, cut], s_full.at[cut], load_sem.at[7 + i]))
     for load in loads:
         load.start()
 
@@ -73,8 +77,8 @@
     for step in range(1, n_chip):
         greet(in_b(step))
 
-    loads[0].wait()
-    loads[1].wait()
+    for load in loads[:7]:
+        load.wait()
     scale = [precond[0:1, BR * i : BR * (i + 1)] for i in range(2)]
     leak = [sink[0:1, BR * i : BR * (i + 1)] for i in range(2)]
     for i in range(2):
@@ -192,7 +196,7 @@
 
     halo_copies = send_halo(0)
     for i in range(6):
-        loads[2 + i].wait()
+        loads[7 + i].wait()
         cut = pl.ds(rows * i, rows)
         high, low = split(s_full[cut])
         s_high[cut] = high
@@ -265,8 +269,7 @@
 def solution(mesh):
     n_board, n_sub = mesh.shape["board"], mesh.shape["sub"]
     vmem = pl.BlockSpec(memory_space=pltpu.VMEM)
-    anywhere = pl.BlockSpec(memory_space=pl.ANY)
-    smem = pl.BlockSpec(memory_space=pltpu.SMEM)
+    hbm = pl.BlockSpec(memory_space=pltpu.HBM)
 
     def on_device(rhs, schur, block_list, pad_rows, pad_cond, sink, precond):
         cases, owned = rhs.shape[1:]
@@ -278,9 +281,14 @@
         return pl.pallas_call(
             functools.partial(kernel, n_board, n_sub),
             out_shape=(out, out),
-            in_specs=[anywhere, anywhere, smem, vmem, vmem, vmem, vmem],
+            in_specs=[hbm] * 7,
             out_specs=(vmem, vmem),
             scratch_shapes=[
+                pltpu.SMEM(block_list.shape, jnp.int32),
+                pltpu.VMEM(pad_rows.shape, jnp.int32),
+                pltpu.VMEM(pad_cond.shape, F32),
+                pltpu.VMEM(sink.shape, F32),
+                pltpu.VMEM(precond.shape, F32),
                 pltpu.VMEM((2, cases, BR), F32),
                 pltpu.VMEM((inner, inner), F32),
                 pltpu.VMEM((inner, inner), BF16),
@@ -288,7 +296,6 @@
                 pltpu.VMEM((owned, BR), BF16),
                 pltpu.VMEM((2, cases + 8, BR), F32),
                 pltpu.VMEM((2, cases + 8, BR), F32),
-                pltpu.VMEM((cases, BR), F32),
                 pltpu.VMEM((2, span, cases, BR), F32),
                 pltpu.VMEM((block_list.shape[1] + 1, cases, BR), F32),
                 pltpu.VMEM((2, span, cases, BR), F32),
@@ -296,7 +303,7 @@
                 pltpu.VMEM((2, cases, BR), F32),
                 pltpu.VMEM((2, 2 * n_board, 1, 128), F32),
                 pltpu.VMEM((2, n_sub // 2, 1, 128), F32),
-                dma((8,)),
+                dma((13,)),
                 dma((2, n_off)), dma((2, n_off)),
                 dma((2, n_off)), dma((2, n_off)),
                 dma((2,)), dma((2,)),
@@ -304,7 +311,7 @@
                 dma((2, n_sub // 2 - 1)), dma((2, n_sub // 2 - 1)),
             ],
             compiler_params=pltpu.CompilerParams(
-                collective_id=0, has_side_effects=True, vmem_limit_bytes=32 * 1024 * 1024
+                collective_id=0, has_side_effects=True, vmem_limit_bytes=67043328
             ),
         )(rhs, schur, block_list, pad_rows, pad_cond, sink, precond)
 

time: 55.1 us -> 49.9 us (0.906)
  local copies, waits for them, and re-layouts: 6.97 us -> 2.75 us
  Pallas kernels: 47.2 us -> 46.3 us
    unnamed x16 -> x2, local copies, waits for them, and re-layouts: 6.97 us -> 2.75 us
    pallas_call x1, Pallas kernels: 47.2 us -> 46.3 us  [on_device(): pl.pallas_call(functools.partial(kernel, n_board, n_sub), out_shape=(out,...]
where the time goes in v2:
time: 49.9 us; the launch traced here: 49.6 us
  Pallas kernels  46.3 us (93%)
  local copies, waits for them, and re-layouts  2.75 us (6%)
  between operations  0.64 us (1%)
    pallas_call x1, Pallas kernels, on_device(): pl.pallas_call(functools.partial(kernel, n_board, n_sub), out_shape=(out,...  46.3 us
    unnamed x2, local copies, waits for them, and re-layouts  2.75 us

profile of v2, /device:TPU:1, one launch (start us, length us, event | category | flops | bytes accessed | tf_op | source)
XLA Modules:
  0.0 49.6 jit_solution(4705160018005176854)
XLA Ops:
  0.6 46.3 %shard_map.86 = (f32[1,32,256]{2,1,0:T(8,128)}, f32[1,32,256]{2,1,0:T(8,128)}) custom-call(f32[1,32,256]{2,1,0:T(8,128)} %rhs.1, f32[1,768,768]{2,1,0:T(8,128)} %schur.1, s32[1,6]{1,0:T(1,128)} %blocks_in.1, s32[1,64]{1,0:T(1,128)} %pad_rows_in.1, f32[1,64]{1,0:T(1,128)} %pad_cond_in.1, f32[1,256]{1,0:T(1,128)} %sink_in.1, f32[1,256]{1,0:T(1,128)} %precond_in.1), custom_call_target="tpu_custom_call" | custom-call | tf_op jit(solution)/shard_map/pallas_call | solution.py:281
  46.9 1.4 %copy.11 = f32[1,32,256]{2,1,0:T(8,128)} copy(f32[1,32,256]{2,1,0:T(8,128)} %get-tuple-element.4) | data formatting | bytes 65536
  48.3 1.4 %copy.12 = f32[1,32,256]{2,1,0:T(8,128)} copy(f32[1,32,256]{2,1,0:T(8,128)} %get-tuple-element.5) | data formatting | bytes 65536

commit v3 on v2

v3 whole, which is shorter than its diff:
```python
import functools

import jax
import jax.numpy as jnp
from jax import lax
from jax.experimental import pallas as pl
from jax.experimental.pallas import tpu as pltpu
from jax.sharding import PartitionSpec as P

BR = 128
REACH = 3
OFFSETS = (3, -3, 2, -2, 1, -1)
F32 = jnp.float32
BF16 = jnp.bfloat16


def split(value):
    high = value.astype(BF16)
    low = (value - high.astype(F32)).astype(BF16)
    return high, low


def bits(count):
    return count.bit_length() - 1


RING4 = (0, 1, 2, 1)
RING8 = (0, 1, 2, 2, 4, 3, 2, 2)


def far_first(count, hops):
    return sorted(range(1, count), key=lambda step: -hops(step))


class Copy:
    def __init__(self, copy, going, coming):
        self.copy, self.going, self.coming = copy, going, coming

    def when(self, condition, act):
        if condition is None:
            act()
        else:
            pl.when(condition)(act)

    def start(self):
        self.when(self.going, self.copy.start)

    def wait_recv(self):
        self.when(self.coming, self.copy.wait_recv)

    def wait_send(self):
        self.when(self.going, self.copy.wait_send)


def kernel(
    n_board, n_sub,
    rhs, schur, blocks_in, pad_rows_in, pad_cond_in, sink_in, precond_in,
    x_out, r_out,
    blocks, pad_rows, pad_cond, sink, precond,
    b_own, s_full, s_high, s_low, one_hot, pad_out, pad_in,
    halo, prod, parts, back, image_own, group_a, group_b,
    load_sem, halo_send, halo_recv, back_send, back_recv, pad_send, pad_recv,
    a_send, a_recv, b_send, b_recv,
):
    me_b = lax.axis_index("board")
    me_s = lax.axis_index("sub")
    core = lax.rem(me_s, 2)
    chip = lax.div(me_s, 2)
    n_a, n_chip = 2 * n_board, n_sub // 2
    a_id = me_b * 2 + core
    touched = blocks.shape[1]
    inner = schur.shape[1]
    order_a = far_first(n_a, lambda step: RING8[step // 2])
    order_b = far_first(n_chip, lambda step: RING4[step % 4] + RING8[step // 4])

    def near(offset):
        return (me_b, me_s + offset)

    def there(offset):
        if offset > 0:
            return me_s < n_sub - offset
        return me_s >= -offset

    flip_b = [(1 << k) * (1 - 2 * lax.rem(lax.div(me_b, 1 << k), 2)) for k in range(bits(n_board))]
    flip_s = [(1 << k) * (1 - 2 * lax.rem(lax.div(me_s, 1 << k), 2)) for k in range(bits(n_sub))]

    def flipped(me, flips, mask):
        for k, flip in enumerate(flips):
            if mask >> k & 1:
                me = me + flip
        return me

    def in_a(step):
        return (flipped(me_b, flip_b, step >> 1), flipped(me_s, flip_s, step & 1))

    def in_b(step):
        return (me_b, flipped(me_s, flip_s, 2 * step))

    loads = [
        pltpu.make_async_copy(rhs.at[0, :, pl.ds(BR * i, BR)], b_own.at[i], load_sem.at[i])
        for i in range(2)
    ]
    small = ((precond_in, precond), (pad_rows_in, pad_rows), (blocks_in, blocks), (pad_cond_in, pad_cond), (sink_in, sink))
    for i, (source, target) in enumerate(small):
        loads.append(pltpu.make_async_copy(source, target, load_sem.at[2 + i]))
    rows = inner // 6
    for i in range(6):
        cut = pl.ds(rows * i, rows)
        loads.append(pltpu.make_async_copy(schur.at[0, cut], s_full.at[cut], load_sem.at[7 + i]))
    for load in loads:
        load.start()

    barrier = pltpu.get_barrier_semaphore()

    def greet(device):
        pl.semaphore_signal(barrier, inc=1, device_id=device, device_id_type=pl.DeviceIdType.MESH)

    beside = 2 * core - 1
    inside = jnp.logical_and(me_s + beside >= 0, me_s + beside < n_sub)
    for offset in (3, -3):
        pl.when(there(offset))(lambda: greet(near(offset)))
    pl.when(inside)(lambda: greet((me_b, me_s + beside)))
    for step in order_b:
        greet(in_b(step))
    for step in order_a:
        greet(in_a(step))

    for load in loads[:3]:
        load.wait()
    scale = [precond[0:1, BR * i : BR * (i + 1)] for i in range(2)]
    for i in range(2):
        halo[0, 2 * REACH + i] = scale[i] * b_own[i]
    count = inside.astype(jnp.int32) + there(3).astype(jnp.int32) + there(-3).astype(jnp.int32)
    pl.semaphore_wait(barrier, count + n_a - 1 + n_chip - 1)

    sent = []

    def send(source, target, send_sem, recv_sem, device, going=None, coming=None):
        copy = Copy(pltpu.make_async_remote_copy(
            src_ref=source, dst_ref=target, send_sem=send_sem, recv_sem=recv_sem,
            device_id=device, device_id_type=pl.DeviceIdType.MESH,
        ), going, coming)
        copy.start()
        sent.append(copy)
        return copy

    def send_halo(slot):
        copies = []
        for n, offset in enumerate(OFFSETS):
            copies.append(send(
                halo.at[slot, pl.ds(2 * REACH, 2)], halo.at[slot, pl.ds(2 * (REACH - offset), 2)],
                halo_send.at[slot, n], halo_recv.at[slot, n], near(offset), there(offset), there(-offset)))
        return copies

    def send_pads(slot):
        return send(pad_out.at[slot], pad_in.at[slot], pad_send.at[slot], pad_recv.at[slot], in_a(2))

    def pads_of(slot):
        high, low = split(jnp.concatenate([halo[slot, 2 * REACH], halo[slot, 2 * REACH + 1]], axis=1))
        both = jnp.dot(jnp.concatenate([high, low], axis=0), one_hot[...], preferred_element_type=F32)
        return both[:32] + both[32:]

    def send_back(slot):
        copies = []
        for n, offset in enumerate(OFFSETS):
            copies.append(send(
                parts.at[slot, pl.ds(2 * (REACH + offset), 2)], back.at[slot, n],
                back_send.at[slot, n], back_recv.at[slot, n], near(offset), there(offset), there(-offset)))
        return copies

    def apply(slot):
        picked = [halo[slot, index[j]] for j in range(touched)]
        splits = [split(block) for block in picked]
        high = jnp.concatenate([pair[0] for pair in splits], axis=1)
        low = jnp.concatenate([pair[1] for pair in splits], axis=1)
        both = jnp.dot(jnp.concatenate([high, low], axis=0), s_high[...], preferred_element_type=F32)
        product = both[:32] + both[32:] + jnp.dot(high, s_low[...], preferred_element_type=F32)
        return picked, [product[:, BR * j : BR * (j + 1)] for j in range(touched)]

    def put_parts(slot, product):
        for j in range(touched):
            prod[j] = product[j]
        for k in range(2 * (2 * REACH + 1)):
            parts[slot, k] = prod[inverse[k]]

    def collect(slot, copies, coupling):
        high, low = split(coupling)
        both = lax.dot_general(
            jnp.concatenate([high, low], axis=0), one_hot[...], (((1,), (1,)), ((), ())), preferred_element_type=F32)
        spread = both[:32] + both[32:]
        for copy in copies:
            copy.wait_recv()
        result = []
        for i in range(2):
            total = parts[slot, 2 * REACH + i]
            for n in range(len(OFFSETS)):
                total = total + back[slot, n, i]
            total = total + spread[:, BR * i : BR * (i + 1)]
            result.append(total + leak[i] * halo[slot, 2 * REACH + i])
        return result

    halo_copies = send_halo(0)
    for load in loads[3:7]:
        load.wait()
    leak = [sink[0:1, BR * i : BR * (i + 1)] for i in range(2)]
    n_pads = pad_rows.shape[1]
    row_ids = lax.broadcasted_iota(jnp.int32, (2 * BR, n_pads), 0)
    one_hot[...] = jnp.zeros_like(one_hot)
    one_hot[:, :n_pads] = jnp.where(row_ids == pad_rows[...], 1.0, 0.0).astype(BF16)
    own_pads = pads_of(0)
    pad_out[...] = jnp.zeros_like(pad_out)
    pad_out[0, :32] = own_pads
    pad_out[0, 32:33, :n_pads] = pad_cond[...]
    pads_copy = send_pads(0)
    last = 2 * (2 * REACH + 1) - 1
    index = [jnp.clip(blocks[0, j] - (me_s - REACH) * 2, 0, last) for j in range(touched)]
    inverse = []
    for k in range(last + 1):
        where = jnp.int32(touched)
        for j in range(touched):
            where = jnp.where(index[j] == k, j, where)
        inverse.append(where)
    prod[touched] = jnp.zeros_like(prod[touched])

    for n, offset in enumerate(OFFSETS):
        @pl.when(jnp.logical_not(there(-offset)))
        def _():
            for slot in range(2):
                back[slot, n] = jnp.zeros_like(back[slot, n])
                halo[slot, 2 * (REACH - offset) : 2 * (REACH - offset) + 2] = jnp.zeros((2, 32, BR), F32)

    for i in range(6):
        loads[7 + i].wait()
        cut = pl.ds(rows * i, rows)
        high, low = split(s_full[cut])
        s_high[cut] = high
        s_low[cut] = low
    for copy in halo_copies:
        copy.wait_recv()
    picked, product = apply(0)
    put_parts(0, product)
    back_copies = send_back(0)
    pads_copy.wait_recv()
    mean_cond = 0.5 * (pad_out[0, 32:33] + pad_in[0, 32:33])
    image = collect(0, back_copies, mean_cond * (own_pads - pad_in[0, :32]))

    for i in range(2):
        image_own[i] = image[i]
        halo[1, 2 * REACH + i] = scale[i] * image[i]
    halo_copies = send_halo(1)
    own_pads = pads_of(1)
    pad_out[1, :32] = own_pads
    pads_copy = send_pads(1)
    moments = [jnp.zeros((32, BR), F32)] * 4
    for i in range(2):
        old, u = halo[0, 2 * REACH + i], halo[1, 2 * REACH + i]
        moments = [
            moments[0] + b_own[i] * old,
            moments[1] + old * image[i],
            moments[2] + u * image[i],
            moments[3] + leak[i] * u * u,
        ]
    pads_copy.wait_recv()
    coupling = mean_cond * (own_pads - pad_in[1, :32])
    moments[3] = moments[3] + own_pads * coupling
    for copy in halo_copies:
        copy.wait_recv()
    picked, product = apply(1)
    for j in range(touched):
        moments[3] = moments[3] + picked[j] * product[j]

    group_a[a_id] = jnp.sum(jnp.concatenate(moments, axis=0).T, axis=0, keepdims=True)
    copies = [
        send(group_a.at[a_id], group_a.at[a_id], a_send.at[step - 1], a_recv.at[step - 1], in_a(step))
        for step in order_a
    ]
    put_parts(1, product)
    back_copies = send_back(1)
    for copy in copies:
        copy.wait_recv()
    group_b[chip] = jnp.sum(group_a[...], axis=0)
    copies = [
        send(group_b.at[chip], group_b.at[chip], b_send.at[step - 1], b_recv.at[step - 1], in_b(step))
        for step in order_b
    ]
    image_u = collect(1, back_copies, coupling)
    for copy in copies:
        copy.wait_recv()
    total = jnp.broadcast_to(jnp.sum(group_b[...], axis=0), (128, 128)).T
    m0, m1, m2, m3 = [total[32 * k : 32 * (k + 1)] for k in range(4)]
    alpha0 = m0 / m1
    cross = m1 - alpha0 * m2
    fresh = (m0 - alpha0 * m1) - alpha0 * cross
    beta = fresh / m0
    bend = cross - alpha0 * (m2 - alpha0 * m3)
    alpha1 = fresh / (bend + beta * (2.0 * cross + beta * m1))
    for i in range(2):
        old = halo[0, 2 * REACH + i]
        residual = b_own[i] - alpha0 * image_own[i]
        direction = scale[i] * residual + beta * old
        image1 = (image_own[i] - alpha0 * image_u[i]) + beta * image_own[i]
        x_out[0, :, BR * i : BR * (i + 1)] = alpha0 * old + alpha1 * direction
        r_out[0, :, BR * i : BR * (i + 1)] = residual - alpha1 * image1
    for copy in sent:
        copy.wait_send()


def put_out(x_in, r_in, x_out, r_out, sem):
    copies = [
        pltpu.make_async_copy(x_in, x_out, sem.at[0]),
        pltpu.make_async_copy(r_in, r_out, sem.at[1]),
    ]
    for copy in copies:
        copy.start()
    for copy in copies:
        copy.wait()


def solution(mesh):
    n_board, n_sub = mesh.shape["board"], mesh.shape["sub"]
    vmem = pl.BlockSpec(memory_space=pltpu.VMEM)
    hbm = pl.BlockSpec(memory_space=pltpu.HBM)

    def on_device(rhs, schur, block_list, pad_rows, pad_cond, sink, precond):
        cases, owned = rhs.shape[1:]
        inner = schur.shape[1]
        n_off = len(OFFSETS)
        span = 2 * (2 * REACH + 1)
        dma = pltpu.SemaphoreType.DMA
        out = jax.ShapeDtypeStruct(rhs.shape, F32)
        results = pl.pallas_call(
            functools.partial(kernel, n_board, n_sub),
            out_shape=(out, out),
            in_specs=[hbm] * 7,
            out_specs=(vmem, vmem),
            scratch_shapes=[
                pltpu.SMEM(block_list.shape, jnp.int32),
                pltpu.VMEM(pad_rows.shape, jnp.int32),
                pltpu.VMEM(pad_cond.shape, F32),
                pltpu.VMEM(sink.shape, F32),
                pltpu.VMEM(precond.shape, F32),
                pltpu.VMEM((2, cases, BR), F32),
                pltpu.VMEM((inner, inner), F32),
                pltpu.VMEM((inner, inner), BF16),
                pltpu.VMEM((inner, inner), BF16),
                pltpu.VMEM((owned, BR), BF16),
                pltpu.VMEM((2, cases + 8, BR), F32),
                pltpu.VMEM((2, cases + 8, BR), F32),
                pltpu.VMEM((2, span, cases, BR), F32),
                pltpu.VMEM((block_list.shape[1] + 1, cases, BR), F32),
                pltpu.VMEM((2, span, cases, BR), F32),
                pltpu.VMEM((2, n_off, 2, cases, BR), F32),
                pltpu.VMEM((2, cases, BR), F32),
                pltpu.VMEM((2 * n_board, 1, 128), F32),
                pltpu.VMEM((n_sub // 2, 1, 128), F32),
                dma((13,)),
                dma((2, n_off)), dma((2, n_off)),
                dma((2, n_off)), dma((2, n_off)),
                dma((2,)), dma((2,)),
                dma((2 * n_board - 1,)), dma((2 * n_board - 1,)),
                dma((n_sub // 2 - 1,)), dma((n_sub // 2 - 1,)),
            ],
            compiler_params=pltpu.CompilerParams(
                collective_id=0, has_side_effects=True, vmem_limit_bytes=32 * 1024 * 1024
            ),
        )(*[pltpu.with_memory_space_constraint(a, pltpu.HBM) for a in (rhs, schur, block_list, pad_rows, pad_cond, sink, precond)])
        return pl.pallas_call(
            put_out,
            out_shape=(out, out),
            in_specs=[vmem, vmem],
            out_specs=(hbm, hbm),
            scratch_shapes=[dma((2,))],
            compiler_params=pltpu.CompilerParams(vmem_limit_bytes=8 * 1024 * 1024),
        )(*results)

    row = P("board", "sub")
    return jax.shard_map(
        on_device,
        mesh=mesh,
        in_specs=(P("board", None, "sub"), P("board", "sub", None), row, row, row, row, row),
        out_specs=(P("board", None, "sub"), P("board", None, "sub")),
        check_vma=False,
    )
```

time: 49.9 us -> 44.7 us (0.90)
  local copies, waits for them, and re-layouts: 2.75 us -> 0 us
  Pallas kernels: 46.3 us -> 44 us
    pallas_call x1, Pallas kernels: 46.3 us -> 43.3 us  [on_device(): pl.pallas_call(functools.partial(kernel, n_board, n_sub), out_shape=(out,...]
    unnamed x2 -> x0, local copies, waits for them, and re-layouts: 2.75 us -> none
    pallas_call x0 -> x1, Pallas kernels: none -> 0.65 us  [on_device(): pl.pallas_call(put_out, out_shape=(out, out), in_specs=[vmem, vmem], out_...]
where the time goes in v3:
time: 44.7 us; the launch traced here: 44.6 us
  Pallas kernels  44 us (98%)
  between operations  0.64 us (1%)
    pallas_call x1, Pallas kernels, on_device(): pl.pallas_call(functools.partial(kernel, n_board, n_sub), out_shape=(out,...  43.3 us

profile of v3, /device:TPU:1, one launch (start us, length us, event | category | flops | bytes accessed | tf_op | source)
XLA Modules:
  0.0 44.6 jit_solution(15994320644474139169)
XLA Ops:
  0.6 43.3 %shard_map.86 = (f32[1,32,256]{2,1,0:T(8,128)S(1)}, f32[1,32,256]{2,1,0:T(8,128)S(1)}) custom-call(f32[1,32,256]{2,1,0:T(8,128)} %rhs.1, f32[1,768,768]{2,1,0:T(8,128)} %schur.1, s32[1,6]{1,0:T(1,128)} %blocks_in.1, s32[1,64]{1,0:T(1,128)} %pad_rows_in.1, f32[1,64]{1,0:T(1,128)} %pad_cond_in.1, f32[1,256]{1,0:T(1,128)} %sink_in.1, f32[1,256]{1,0:T(1,128)} %precond_in.1), custom_call_target="tpu_custom_call" | custom-call | tf_op jit(solution)/shard_map/pallas_call | solution.py:331
  44.0 0.6 %shard_map.87 = (f32[1,32,256]{2,1,0:T(8,128)}, f32[1,32,256]{2,1,0:T(8,128)}) custom-call(f32[1,32,256]{2,1,0:T(8,128)S(1)} %get-tuple-element.4.x_in, f32[1,32,256]{2,1,0:T(8,128)S(1)} %get-tuple-element.5.r_in), custom_call_target="tpu_custom_call" | custom-call | tf_op jit(solution)/shard_map/pallas_call | solution.py:367

commit v4 on v3

--- a/solution.py
+++ b/solution.py
@@ -60,7 +60,7 @@
     b_own, s_full, s_high, s_low, one_hot, pad_out, pad_in,
     halo, prod, parts, back, image_own, group_a, group_b,
     load_sem, halo_send, halo_recv, back_send, back_recv, pad_send, pad_recv,
-    a_send, a_recv, b_send, b_recv,
+    a_send, a_recv, b_send, b_recv, relay,
 ):
     me_b = lax.axis_index("board")
     me_s = lax.axis_index("sub")
@@ -95,6 +95,14 @@
 
     def in_b(step):
         return (me_b, flipped(me_s, flip_s, 2 * step))
+
+    def steps(count):
+        return sorted({step % count for step in (1, -1, 2, -2)} - {0})
+
+    layer = 8
+    ring_b = [(lax.rem(me_b + step, n_board), me_s) for step in steps(n_board)]
+    ring_s = [(me_b, lax.rem(me_s + layer * step, n_sub)) for step in steps(n_sub // layer)]
+    row = [in_b(step) for step in range(1, layer // 2)]
 
     loads = [
         pltpu.make_async_copy(rhs.at[0, :, pl.ds(BR * i, BR)], b_own.at[i], load_sem.at[i])
@@ -115,23 +123,26 @@
     def greet(device):
         pl.semaphore_signal(barrier, inc=1, device_id=device, device_id_type=pl.DeviceIdType.MESH)
 
-    beside = 2 * core - 1
-    inside = jnp.logical_and(me_s + beside >= 0, me_s + beside < n_sub)
-    for offset in (3, -3):
+    count = len(ring_b) + len(ring_s) + len(row)
+    for offset in OFFSETS:
         pl.when(there(offset))(lambda: greet(near(offset)))
-    pl.when(inside)(lambda: greet((me_b, me_s + beside)))
-    for step in order_b:
-        greet(in_b(step))
-    for step in order_a:
-        greet(in_a(step))
+        count = count + there(offset).astype(jnp.int32)
+    for device in row + ring_b + ring_s:
+        greet(device)
 
     for load in loads[:3]:
         load.wait()
     scale = [precond[0:1, BR * i : BR * (i + 1)] for i in range(2)]
     for i in range(2):
         halo[0, 2 * REACH + i] = scale[i] * b_own[i]
-    count = inside.astype(jnp.int32) + there(3).astype(jnp.int32) + there(-3).astype(jnp.int32)
-    pl.semaphore_wait(barrier, count + n_a - 1 + n_chip - 1)
+    pl.semaphore_wait(barrier, count)
+
+    def pass_on(turn):
+        for device in ring_b + ring_s:
+            pl.semaphore_signal(relay.at[turn], inc=1, device_id=device, device_id_type=pl.DeviceIdType.MESH)
+
+    def hear(turn):
+        pl.semaphore_wait(relay.at[turn], len(ring_b) + len(ring_s))
 
     sent = []
 
@@ -200,6 +211,7 @@
         return result
 
     halo_copies = send_halo(0)
+    pass_on(0)
     for load in loads[3:7]:
         load.wait()
     leak = [sink[0:1, BR * i : BR * (i + 1)] for i in range(2)]
@@ -240,6 +252,8 @@
     picked, product = apply(0)
     put_parts(0, product)
     back_copies = send_back(0)
+    hear(0)
+    pass_on(1)
     pads_copy.wait_recv()
     mean_cond = 0.5 * (pad_out[0, 32:33] + pad_in[0, 32:33])
     image = collect(0, back_copies, mean_cond * (own_pads - pad_in[0, :32]))
@@ -268,6 +282,8 @@
     picked, product = apply(1)
     for j in range(touched):
         moments[3] = moments[3] + picked[j] * product[j]
+
+    hear(1)
 
     group_a[a_id] = jnp.sum(jnp.concatenate(moments, axis=0).T, axis=0, keepdims=True)
     copies = [
@@ -359,6 +375,7 @@
                 dma((2,)), dma((2,)),
                 dma((2 * n_board - 1,)), dma((2 * n_board - 1,)),
                 dma((n_sub // 2 - 1,)), dma((n_sub // 2 - 1,)),
+                pltpu.SemaphoreType.REGULAR((2,)),
             ],
             compiler_params=pltpu.CompilerParams(
                 collective_id=0, has_side_effects=True, vmem_limit_bytes=32 * 1024 * 1024

time: 44.7 us -> 42.8 us (0.957)
  Pallas kernels: 44 us -> 42.1 us
    pallas_call x1, Pallas kernels: 43.3 us -> 41.4 us  [on_device(): pl.pallas_call(functools.partial(kernel, n_board, n_sub), out_shape=(out,...]
where the time goes in v4:
time: 42.8 us; the launch traced here: 42.7 us
  Pallas kernels  42.1 us (98%)
  between operations  0.64 us (1%)
    pallas_call x1, Pallas kernels, on_device(): pl.pallas_call(functools.partial(kernel, n_board, n_sub), out_shape=(out,...  41.4 us

profile of v4, /device:TPU:1, one launch (start us, length us, event | category | flops | bytes accessed | tf_op | source)
XLA Modules:
  0.0 42.7 jit_solution(5067962995234162872)
XLA Ops:
  0.6 41.4 %shard_map.86 = (f32[1,32,256]{2,1,0:T(8,128)S(1)}, f32[1,32,256]{2,1,0:T(8,128)S(1)}) custom-call(f32[1,32,256]{2,1,0:T(8,128)} %rhs.1, f32[1,768,768]{2,1,0:T(8,128)} %schur.1, s32[1,6]{1,0:T(1,128)} %blocks_in.1, s32[1,64]{1,0:T(1,128)} %pad_rows_in.1, f32[1,64]{1,0:T(1,128)} %pad_cond_in.1, f32[1,256]{1,0:T(1,128)} %sink_in.1, f32[1,256]{1,0:T(1,128)} %precond_in.1), custom_call_target="tpu_custom_call" | custom-call | tf_op jit(solution)/shard_map/pallas_call | solution.py:347
  42.0 0.6 %shard_map.87 = (f32[1,32,256]{2,1,0:T(8,128)}, f32[1,32,256]{2,1,0:T(8,128)}) custom-call(f32[1,32,256]{2,1,0:T(8,128)S(1)} %get-tuple-element.4.x_in, f32[1,32,256]{2,1,0:T(8,128)S(1)} %get-tuple-element.5.r_in), custom_call_target="tpu_custom_call" | custom-call | tf_op jit(solution)/shard_map/pallas_call | solution.py:384

commit v5 on v4

--- a/solution.py
+++ b/solution.py
@@ -104,6 +104,18 @@
     ring_s = [(me_b, lax.rem(me_s + layer * step, n_sub)) for step in steps(n_sub // layer)]
     row = [in_b(step) for step in range(1, layer // 2)]
 
+    barrier = pltpu.get_barrier_semaphore()
+
+    def greet(device):
+        pl.semaphore_signal(barrier, inc=1, device_id=device, device_id_type=pl.DeviceIdType.MESH)
+
+    count = len(ring_b) + len(ring_s) + len(row)
+    for offset in OFFSETS:
+        pl.when(there(offset))(lambda: greet(near(offset)))
+        count = count + there(offset).astype(jnp.int32)
+    for device in row + ring_b + ring_s:
+        greet(device)
+
     loads = [
         pltpu.make_async_copy(rhs.at[0, :, pl.ds(BR * i, BR)], b_own.at[i], load_sem.at[i])
         for i in range(2)
@@ -118,18 +130,6 @@
     for load in loads:
         load.start()
 
-    barrier = pltpu.get_barrier_semaphore()
-
-    def greet(device):
-        pl.semaphore_signal(barrier, inc=1, device_id=device, device_id_type=pl.DeviceIdType.MESH)
-
-    count = len(ring_b) + len(ring_s) + len(row)
-    for offset in OFFSETS:
-        pl.when(there(offset))(lambda: greet(near(offset)))
-        count = count + there(offset).astype(jnp.int32)
-    for device in row + ring_b + ring_s:
-        greet(device)
-
     for load in loads[:3]:
         load.wait()
     scale = [precond[0:1, BR * i : BR * (i + 1)] for i in range(2)]
@@ -154,6 +154,18 @@
         copy.start()
         sent.append(copy)
         return copy
+
+    def spread_row(group, me, send_sem, recv_sem, devices):
+        for device in devices:
+            pltpu.make_async_remote_copy(
+                src_ref=group.at[me], dst_ref=group.at[me], send_sem=send_sem, recv_sem=recv_sem,
+                device_id=device, device_id_type=pl.DeviceIdType.MESH,
+            ).start()
+        others = group.at[pl.ds(0, len(devices))]
+        return pltpu.make_async_remote_copy(
+            src_ref=others, dst_ref=others, send_sem=send_sem, recv_sem=recv_sem,
+            device_id=devices[0], device_id_type=pl.DeviceIdType.MESH,
+        )
 
     def send_halo(slot):
         copies = []
@@ -286,22 +298,17 @@
     hear(1)
 
     group_a[a_id] = jnp.sum(jnp.concatenate(moments, axis=0).T, axis=0, keepdims=True)
-    copies = [
-        send(group_a.at[a_id], group_a.at[a_id], a_send.at[step - 1], a_recv.at[step - 1], in_a(step))
-        for step in order_a
-    ]
+    rows_a = spread_row(group_a, a_id, a_send, a_recv, [in_a(step) for step in order_a])
     put_parts(1, product)
     back_copies = send_back(1)
-    for copy in copies:
-        copy.wait_recv()
+    rows_a.wait_recv()
     group_b[chip] = jnp.sum(group_a[...], axis=0)
-    copies = [
-        send(group_b.at[chip], group_b.at[chip], b_send.at[step - 1], b_recv.at[step - 1], in_b(step))
-        for step in order_b
-    ]
+    rows_b = spread_row(group_b, chip, b_send, b_recv, [in_b(step) for step in order_b])
     image_u = collect(1, back_copies, coupling)
-    for copy in copies:
-        copy.wait_recv()
+    for copy in sent:
+        copy.wait_send()
+    rows_a.wait_send()
+    rows_b.wait_recv()
     total = jnp.broadcast_to(jnp.sum(group_b[...], axis=0), (128, 128)).T
     m0, m1, m2, m3 = [total[32 * k : 32 * (k + 1)] for k in range(4)]
     alpha0 = m0 / m1
@@ -317,8 +324,7 @@
         image1 = (image_own[i] - alpha0 * image_u[i]) + beta * image_own[i]
         x_out[0, :, BR * i : BR * (i + 1)] = alpha0 * old + alpha1 * direction
         r_out[0, :, BR * i : BR * (i + 1)] = residual - alpha1 * image1
-    for copy in sent:
-        copy.wait_send()
+    rows_b.wait_send()
 
 
 def put_out(x_in, r_in, x_out, r_out, sem):
@@ -373,8 +379,8 @@
                 dma((2, n_off)), dma((2, n_off)),
                 dma((2, n_off)), dma((2, n_off)),
                 dma((2,)), dma((2,)),
-                dma((2 * n_board - 1,)), dma((2 * n_board - 1,)),
-                dma((n_sub // 2 - 1,)), dma((n_sub // 2 - 1,)),
+                dma(()), dma(()),
+                dma(()), dma(()),
                 pltpu.SemaphoreType.REGULAR((2,)),
             ],
             compiler_params=pltpu.CompilerParams(

time: 42.8 us -> 41.9 us (0.979)
  Pallas kernels: 42.1 us -> 41.1 us
    pallas_call x1, Pallas kernels: 41.4 us -> 40.5 us  [on_device(): pl.pallas_call(functools.partial(kernel, n_board, n_sub), out_shape=(out,...]
where the time goes in v5:
time: 41.9 us; the launch traced here: 41.7 us
  Pallas kernels  41.1 us (98%)
  between operations  0.64 us (2%)
    pallas_call x1, Pallas kernels, on_device(): pl.pallas_call(functools.partial(kernel, n_board, n_sub), out_shape=(out,...  40.5 us

profile of v5, /device:TPU:1, one launch (start us, length us, event | category | flops | bytes accessed | tf_op | source)
XLA Modules:
  0.0 41.7 jit_solution(2416591945305524236)
XLA Ops:
  0.6 40.5 %shard_map.86 = (f32[1,32,256]{2,1,0:T(8,128)S(1)}, f32[1,32,256]{2,1,0:T(8,128)S(1)}) custom-call(f32[1,32,256]{2,1,0:T(8,128)} %rhs.1, f32[1,768,768]{2,1,0:T(8,128)} %schur.1, s32[1,6]{1,0:T(1,128)} %blocks_in.1, s32[1,64]{1,0:T(1,128)} %pad_rows_in.1, f32[1,64]{1,0:T(1,128)} %pad_cond_in.1, f32[1,256]{1,0:T(1,128)} %sink_in.1, f32[1,256]{1,0:T(1,128)} %precond_in.1), custom_call_target="tpu_custom_call" | custom-call | tf_op jit(solution)/shard_map/pallas_call | solution.py:353
  41.1 0.6 %shard_map.87 = (f32[1,32,256]{2,1,0:T(8,128)}, f32[1,32,256]{2,1,0:T(8,128)}) custom-call(f32[1,32,256]{2,1,0:T(8,128)S(1)} %get-tuple-element.4.x_in, f32[1,32,256]{2,1,0:T(8,128)S(1)} %get-tuple-element.5.r_in), custom_call_target="tpu_custom_call" | custom-call | tf_op jit(solution)/shard_map/pallas_call | solution.py:390

commit v6 on v5

--- a/solution.py
+++ b/solution.py
@@ -9,6 +9,7 @@
 
 BR = 128
 REACH = 3
+HALF = 16
 OFFSETS = (3, -3, 2, -2, 1, -1)
 F32 = jnp.float32
 BF16 = jnp.bfloat16
@@ -58,10 +59,11 @@
     x_out, r_out,
     blocks, pad_rows, pad_cond, sink, precond,
     b_own, s_full, s_high, s_low, one_hot, pad_out, pad_in,
-    halo, prod, parts, back, image_own, group_a, group_b,
+    halo_first, halo_second, prod, parts, back, image_own, group_a, group_b,
     load_sem, halo_send, halo_recv, back_send, back_recv, pad_send, pad_recv,
     a_send, a_recv, b_send, b_recv, relay,
 ):
+    halo = (halo_first, halo_second)
     me_b = lax.axis_index("board")
     me_s = lax.axis_index("sub")
     core = lax.rem(me_s, 2)
@@ -134,7 +136,8 @@
         load.wait()
     scale = [precond[0:1, BR * i : BR * (i + 1)] for i in range(2)]
     for i in range(2):
-        halo[0, 2 * REACH + i] = scale[i] * b_own[i]
+        for part in range(2):
+            halo[part][0, 2 * REACH + i] = scale[i] * b_own[i, HALF * part : HALF * (part + 1)]
     pl.semaphore_wait(barrier, count)
 
     def pass_on(turn):
@@ -167,62 +170,66 @@
             device_id=devices[0], device_id_type=pl.DeviceIdType.MESH,
         )
 
-    def send_halo(slot):
-        copies = []
-        for n, offset in enumerate(OFFSETS):
-            copies.append(send(
-                halo.at[slot, pl.ds(2 * REACH, 2)], halo.at[slot, pl.ds(2 * (REACH - offset), 2)],
-                halo_send.at[slot, n], halo_recv.at[slot, n], near(offset), there(offset), there(-offset)))
-        return copies
+    def send_halo(slot, part):
+        return [
+            send(halo[part].at[slot, pl.ds(2 * REACH, 2)], halo[part].at[slot, pl.ds(2 * (REACH - offset), 2)],
+                 halo_send.at[slot, part, n], halo_recv.at[slot, part, n], near(offset), there(offset), there(-offset))
+            for n, offset in enumerate(OFFSETS)
+        ]
 
     def send_pads(slot):
         return send(pad_out.at[slot], pad_in.at[slot], pad_send.at[slot], pad_recv.at[slot], in_a(2))
 
+    def own(slot, i):
+        return jnp.concatenate([halo[part][slot, 2 * REACH + i] for part in range(2)], axis=0)
+
     def pads_of(slot):
-        high, low = split(jnp.concatenate([halo[slot, 2 * REACH], halo[slot, 2 * REACH + 1]], axis=1))
+        high, low = split(jnp.concatenate([own(slot, 0), own(slot, 1)], axis=1))
         both = jnp.dot(jnp.concatenate([high, low], axis=0), one_hot[...], preferred_element_type=F32)
         return both[:32] + both[32:]
 
-    def send_back(slot):
-        copies = []
-        for n, offset in enumerate(OFFSETS):
-            copies.append(send(
-                parts.at[slot, pl.ds(2 * (REACH + offset), 2)], back.at[slot, n],
-                back_send.at[slot, n], back_recv.at[slot, n], near(offset), there(offset), there(-offset)))
-        return copies
-
-    def apply(slot):
-        picked = [halo[slot, index[j]] for j in range(touched)]
+    def send_back(slot, part):
+        return [
+            send(parts.at[slot, part, pl.ds(2 * (REACH + offset), 2)], back.at[slot, part, n],
+                 back_send.at[slot, part, n], back_recv.at[slot, part, n], near(offset), there(offset), there(-offset))
+            for n, offset in enumerate(OFFSETS)
+        ]
+
+    def apply(slot, part):
+        picked = [halo[part][slot, index[j]] for j in range(touched)]
         splits = [split(block) for block in picked]
         high = jnp.concatenate([pair[0] for pair in splits], axis=1)
         low = jnp.concatenate([pair[1] for pair in splits], axis=1)
         both = jnp.dot(jnp.concatenate([high, low], axis=0), s_high[...], preferred_element_type=F32)
-        product = both[:32] + both[32:] + jnp.dot(high, s_low[...], preferred_element_type=F32)
+        product = both[:HALF] + both[HALF:] + jnp.dot(high, s_low[...], preferred_element_type=F32)
         return picked, [product[:, BR * j : BR * (j + 1)] for j in range(touched)]
 
-    def put_parts(slot, product):
+    def put_parts(slot, part, product):
         for j in range(touched):
-            prod[j] = product[j]
+            prod[part, j] = product[j]
         for k in range(2 * (2 * REACH + 1)):
-            parts[slot, k] = prod[inverse[k]]
-
-    def collect(slot, copies, coupling):
+            parts[slot, part, k] = prod[part, inverse[k]]
+
+    def spread_pads(coupling):
         high, low = split(coupling)
         both = lax.dot_general(
             jnp.concatenate([high, low], axis=0), one_hot[...], (((1,), (1,)), ((), ())), preferred_element_type=F32)
-        spread = both[:32] + both[32:]
+        return both[:32] + both[32:]
+
+    def collect(slot, part, copies, spread):
+        cut = slice(HALF * part, HALF * (part + 1))
         for copy in copies:
             copy.wait_recv()
         result = []
         for i in range(2):
-            total = parts[slot, 2 * REACH + i]
+            total = parts[slot, part, 2 * REACH + i]
             for n in range(len(OFFSETS)):
-                total = total + back[slot, n, i]
-            total = total + spread[:, BR * i : BR * (i + 1)]
-            result.append(total + leak[i] * halo[slot, 2 * REACH + i])
+                total = total + back[slot, part, n, i]
+            total = total + spread[cut, BR * i : BR * (i + 1)]
+            result.append(total + leak[i] * halo[part][slot, 2 * REACH + i])
         return result
 
-    halo_copies = send_halo(0)
+    halo_copies = [send_halo(0, part) for part in range(2)]
     pass_on(0)
     for load in loads[3:7]:
         load.wait()
@@ -244,14 +251,17 @@
         for j in range(touched):
             where = jnp.where(index[j] == k, j, where)
         inverse.append(where)
-    prod[touched] = jnp.zeros_like(prod[touched])
+    for part in range(2):
+        prod[part, touched] = jnp.zeros((HALF, BR), F32)
 
     for n, offset in enumerate(OFFSETS):
         @pl.when(jnp.logical_not(there(-offset)))
         def _():
+            nothing = jnp.zeros((2, HALF, BR), F32)
             for slot in range(2):
-                back[slot, n] = jnp.zeros_like(back[slot, n])
-                halo[slot, 2 * (REACH - offset) : 2 * (REACH - offset) + 2] = jnp.zeros((2, 32, BR), F32)
+                for part in range(2):
+                    back[slot, part, n] = nothing
+                    halo[part][slot, 2 * (REACH - offset) : 2 * (REACH - offset) + 2] = nothing
 
     for i in range(6):
         loads[7 + i].wait()
@@ -259,52 +269,64 @@
         high, low = split(s_full[cut])
         s_high[cut] = high
         s_low[cut] = low
-    for copy in halo_copies:
-        copy.wait_recv()
-    picked, product = apply(0)
-    put_parts(0, product)
-    back_copies = send_back(0)
+    back_copies = []
+    for part in range(2):
+        for copy in halo_copies[part]:
+            copy.wait_recv()
+        picked, product = apply(0, part)
+        put_parts(0, part, product)
+        back_copies.append(send_back(0, part))
     hear(0)
     pass_on(1)
     pads_copy.wait_recv()
     mean_cond = 0.5 * (pad_out[0, 32:33] + pad_in[0, 32:33])
-    image = collect(0, back_copies, mean_cond * (own_pads - pad_in[0, :32]))
-
-    for i in range(2):
-        image_own[i] = image[i]
-        halo[1, 2 * REACH + i] = scale[i] * image[i]
-    halo_copies = send_halo(1)
+    spread = spread_pads(mean_cond * (own_pads - pad_in[0, :32]))
+
+    halo_copies = []
+    for part in range(2):
+        cut = slice(HALF * part, HALF * (part + 1))
+        image = collect(0, part, back_copies[part], spread)
+        for i in range(2):
+            image_own[i, cut] = image[i]
+            halo[part][1, 2 * REACH + i] = scale[i] * image[i]
+        halo_copies.append(send_halo(1, part))
     own_pads = pads_of(1)
     pad_out[1, :32] = own_pads
     pads_copy = send_pads(1)
     moments = [jnp.zeros((32, BR), F32)] * 4
     for i in range(2):
-        old, u = halo[0, 2 * REACH + i], halo[1, 2 * REACH + i]
+        old, u = own(0, i), own(1, i)
         moments = [
             moments[0] + b_own[i] * old,
-            moments[1] + old * image[i],
-            moments[2] + u * image[i],
+            moments[1] + old * image_own[i],
+            moments[2] + u * image_own[i],
             moments[3] + leak[i] * u * u,
         ]
     pads_copy.wait_recv()
     coupling = mean_cond * (own_pads - pad_in[1, :32])
     moments[3] = moments[3] + own_pads * coupling
-    for copy in halo_copies:
-        copy.wait_recv()
-    picked, product = apply(1)
-    for j in range(touched):
-        moments[3] = moments[3] + picked[j] * product[j]
-
+    products, inner_parts = [], []
+    for part in range(2):
+        for copy in halo_copies[part]:
+            copy.wait_recv()
+        picked, product = apply(1, part)
+        products.append(product)
+        inner_parts.append(sum(picked[j] * product[j] for j in range(touched)))
+    moments[3] = moments[3] + jnp.concatenate(inner_parts, axis=0)
     hear(1)
 
     group_a[a_id] = jnp.sum(jnp.concatenate(moments, axis=0).T, axis=0, keepdims=True)
     rows_a = spread_row(group_a, a_id, a_send, a_recv, [in_a(step) for step in order_a])
-    put_parts(1, product)
-    back_copies = send_back(1)
+    back_copies = []
+    for part in range(2):
+        put_parts(1, part, products[part])
+        back_copies.append(send_back(1, part))
     rows_a.wait_recv()
     group_b[chip] = jnp.sum(group_a[...], axis=0)
     rows_b = spread_row(group_b, chip, b_send, b_recv, [in_b(step) for step in order_b])
-    image_u = collect(1, back_copies, coupling)
+    spread = spread_pads(coupling)
+    halves = [collect(1, part, back_copies[part], spread) for part in range(2)]
+    image_u = [jnp.concatenate([half[i] for half in halves], axis=0) for i in range(2)]
     for copy in sent:
         copy.wait_send()
     rows_a.wait_send()
@@ -318,7 +340,7 @@
     bend = cross - alpha0 * (m2 - alpha0 * m3)
     alpha1 = fresh / (bend + beta * (2.0 * cross + beta * m1))
     for i in range(2):
-        old = halo[0, 2 * REACH + i]
+        old = own(0, i)
         residual = b_own[i] - alpha0 * image_own[i]
         direction = scale[i] * residual + beta * old
         image1 = (image_own[i] - alpha0 * image_u[i]) + beta * image_own[i]
@@ -368,16 +390,17 @@
                 pltpu.VMEM((owned, BR), BF16),
                 pltpu.VMEM((2, cases + 8, BR), F32),
                 pltpu.VMEM((2, cases + 8, BR), F32),
-                pltpu.VMEM((2, span, cases, BR), F32),
-                pltpu.VMEM((block_list.shape[1] + 1, cases, BR), F32),
-                pltpu.VMEM((2, span, cases, BR), F32),
-                pltpu.VMEM((2, n_off, 2, cases, BR), F32),
+                pltpu.VMEM((2, span, HALF, BR), F32),
+                pltpu.VMEM((2, span, HALF, BR), F32),
+                pltpu.VMEM((2, block_list.shape[1] + 1, HALF, BR), F32),
+                pltpu.VMEM((2, 2, span, HALF, BR), F32),
+                pltpu.VMEM((2, 2, n_off, 2, HALF, BR), F32),
                 pltpu.VMEM((2, cases, BR), F32),
                 pltpu.VMEM((2 * n_board, 1, 128), F32),
                 pltpu.VMEM((n_sub // 2, 1, 128), F32),
                 dma((13,)),
-                dma((2, n_off)), dma((2, n_off)),
-                dma((2, n_off)), dma((2, n_off)),
+                dma((2, 2, n_off)), dma((2, 2, n_off)),
+                dma((2, 2, n_off)), dma((2, 2, n_off)),
                 dma((2,)), dma((2,)),
                 dma(()), dma(()),
                 dma(()), dma(()),

time: 41.9 us -> 41.5 us (level)
  no operation moved by 1% of the time
where the time goes in v6:
time: 41.5 us; the launch traced here: 41.3 us
  Pallas kernels  40.7 us (98%)
  between operations  0.64 us (2%)
    pallas_call x1, Pallas kernels, on_device(): pl.pallas_call(functools.partial(kernel, n_board, n_sub), out_shape=(out,...  40 us

profile of v6, /device:TPU:1, one launch (start us, length us, event | category | flops | bytes accessed | tf_op | source)
XLA Modules:
  0.0 41.3 jit_solution(11476391966695446317)
XLA Ops:
  0.6 40.0 %shard_map.86 = (f32[1,32,256]{2,1,0:T(8,128)S(1)}, f32[1,32,256]{2,1,0:T(8,128)S(1)}) custom-call(f32[1,32,256]{2,1,0:T(8,128)} %rhs.1, f32[1,768,768]{2,1,0:T(8,128)} %schur.1, s32[1,6]{1,0:T(1,128)} %blocks_in.1, s32[1,64]{1,0:T(1,128)} %pad_rows_in.1, f32[1,64]{1,0:T(1,128)} %pad_cond_in.1, f32[1,256]{1,0:T(1,128)} %sink_in.1, f32[1,256]{1,0:T(1,128)} %precond_in.1), custom_call_target="tpu_custom_call" | custom-call | tf_op jit(solution)/shard_map/pallas_call | solution.py:375
  40.7 0.6 %shard_map.87 = (f32[1,32,256]{2,1,0:T(8,128)}, f32[1,32,256]{2,1,0:T(8,128)}) custom-call(f32[1,32,256]{2,1,0:T(8,128)S(1)} %get-tuple-element.4.x_in, f32[1,32,256]{2,1,0:T(8,128)S(1)} %get-tuple-element.5.r_in), custom_call_target="tpu_custom_call" | custom-call | tf_op jit(solution)/shard_map/pallas_call | solution.py:413

commit v7 on v6

--- a/solution.py
+++ b/solution.py
@@ -161,7 +161,7 @@
     def spread_row(group, me, send_sem, recv_sem, devices):
         for device in devices:
             pltpu.make_async_remote_copy(
-                src_ref=group.at[me], dst_ref=group.at[me], send_sem=send_sem, recv_sem=recv_sem,
+                src_ref=group.at[pl.ds(me, 1)], dst_ref=group.at[pl.ds(me, 1)], send_sem=send_sem, recv_sem=recv_sem,
                 device_id=device, device_id_type=pl.DeviceIdType.MESH,
             ).start()
         others = group.at[pl.ds(0, len(devices))]
@@ -315,14 +315,14 @@
     moments[3] = moments[3] + jnp.concatenate(inner_parts, axis=0)
     hear(1)
 
-    group_a[a_id] = jnp.sum(jnp.concatenate(moments, axis=0).T, axis=0, keepdims=True)
+    group_a[pl.ds(a_id, 1)] = jnp.sum(jnp.concatenate(moments, axis=0).T, axis=0, keepdims=True)
     rows_a = spread_row(group_a, a_id, a_send, a_recv, [in_a(step) for step in order_a])
     back_copies = []
     for part in range(2):
         put_parts(1, part, products[part])
         back_copies.append(send_back(1, part))
     rows_a.wait_recv()
-    group_b[chip] = jnp.sum(group_a[...], axis=0)
+    group_b[pl.ds(chip, 1)] = jnp.sum(group_a[...], axis=0, keepdims=True)
     rows_b = spread_row(group_b, chip, b_send, b_recv, [in_b(step) for step in order_b])
     spread = spread_pads(coupling)
     halves = [collect(1, part, back_copies[part], spread) for part in range(2)]
@@ -331,7 +331,7 @@
         copy.wait_send()
     rows_a.wait_send()
     rows_b.wait_recv()
-    total = jnp.broadcast_to(jnp.sum(group_b[...], axis=0), (128, 128)).T
+    total = jnp.broadcast_to(jnp.sum(group_b[...], axis=0, keepdims=True), (128, 128)).T
     m0, m1, m2, m3 = [total[32 * k : 32 * (k + 1)] for k in range(4)]
     alpha0 = m0 / m1
     cross = m1 - alpha0 * m2
@@ -396,8 +396,8 @@
                 pltpu.VMEM((2, 2, span, HALF, BR), F32),
                 pltpu.VMEM((2, 2, n_off, 2, HALF, BR), F32),
                 pltpu.VMEM((2, cases, BR), F32),
-                pltpu.VMEM((2 * n_board, 1, 128), F32),
-                pltpu.VMEM((n_sub // 2, 1, 128), F32),
+                pltpu.VMEM((2 * n_board, 128), F32),
+                pltpu.VMEM((n_sub // 2, 128), F32),
                 dma((13,)),
                 dma((2, 2, n_off)), dma((2, 2, n_off)),
                 dma((2, 2, n_off)), dma((2, 2, n_off)),

time: 41.5 us -> 41.4 us (level)
  no operation moved by 1% of the time
where the time goes in v7:
time: 41.4 us; the launch traced here: 41.3 us
  Pallas kernels  40.6 us (98%)
  between operations  0.64 us (2%)
    pallas_call x1, Pallas kernels, on_device(): pl.pallas_call(functools.partial(kernel, n_board, n_sub), out_shape=(out,...  40 us

profile of v7, /device:TPU:1, one launch (start us, length us, event | category | flops | bytes accessed | tf_op | source)
XLA Modules:
  0.0 41.3 jit_solution(13138886460260664059)
XLA Ops:
  0.6 40.0 %shard_map.86 = (f32[1,32,256]{2,1,0:T(8,128)S(1)}, f32[1,32,256]{2,1,0:T(8,128)S(1)}) custom-call(f32[1,32,256]{2,1,0:T(8,128)} %rhs.1, f32[1,768,768]{2,1,0:T(8,128)} %schur.1, s32[1,6]{1,0:T(1,128)} %blocks_in.1, s32[1,64]{1,0:T(1,128)} %pad_rows_in.1, f32[1,64]{1,0:T(1,128)} %pad_cond_in.1, f32[1,256]{1,0:T(1,128)} %sink_in.1, f32[1,256]{1,0:T(1,128)} %precond_in.1), custom_call_target="tpu_custom_call" | custom-call | tf_op jit(solution)/shard_map/pallas_call | solution.py:375
  40.6 0.6 %shard_map.87 = (f32[1,32,256]{2,1,0:T(8,128)}, f32[1,32,256]{2,1,0:T(8,128)}) custom-call(f32[1,32,256]{2,1,0:T(8,128)S(1)} %get-tuple-element.4.x_in, f32[1,32,256]{2,1,0:T(8,128)S(1)} %get-tuple-element.5.r_in), custom_call_target="tpu_custom_call" | custom-call | tf_op jit(solution)/shard_map/pallas_call | solution.py:413
